TPU v7x, 32 devices: a whole 2x2x4 slice. The times are simulated.
32 devices in a mesh: dp: 4 (over y, core), seq: 8 (over z, x).
Axes of the slice: x: 2, y: 2, z: 4, core: 2. Of those that a mesh axis runs over, the one named last changes fastest.
Arguments:
- inputs: bfloat16 [4, 1024, 2048], P('dp', 'seq'), may hold values from -6 to 6
- w_query: bfloat16 [2048, 2048], P(None, 'seq'), may hold values from -0.125 to 0.125
- sharpness: float32 [32], P('seq'), may hold values from 0.03 to 0.3
- pattern: int32 [8, 2], replicated, may hold values from 0 to 7, as said below
- lengths: int32 [4], P('dp'), may hold values from 512 to 1024
- probes: bfloat16 [4, 1024, 2048], P('dp', 'seq'), may hold values from -36 to 36
- start_vector: float32 [2048], replicated, may hold values from -6 to 6
Outputs:
- branch: bfloat16 [4, 1024, 2048], P('dp', 'seq')
- probe_vjp: bfloat16 [4, 1024, 2048], P('dp', 'seq')
- logdet_terms: float32 [4, 2], P('dp')
- sharpness_grad: float32 [32], P('seq')
- spec_vector: float32 [2048], replicated
- spec_norm: float32 [1], replicated
Inputs may be any that keep to these rules, and one draw needn't show every extreme that they name: `pattern`: entry 0 of row I is I itself; the 2 entries of a row differ.
All inputs are finite; a program needn't handle non-finite values.
Results may differ from a plain program's by a relative error of at most 0.007.
Values may be sent and summed in bfloat16 or wider, within the bound.
A program may use at most 64 MiB of HBM per device.

v0:
```python
import math

import jax
import jax.numpy as jnp
from jax import lax
from jax.sharding import PartitionSpec as P

DH = 64
INNER = 2048


def head_forward(query_head, sharp_head, pattern, length):
    head_size, seq_total = query_head.shape
    block_count, fanout = pattern.shape
    block_len = seq_total // block_count
    query_tiles = jnp.transpose(query_head.reshape(head_size, block_count, block_len), (1, 0, 2))
    key_tiles = jnp.take(query_tiles, pattern, axis=0)
    query_norms = jnp.sum(jnp.square(query_tiles.astype(jnp.float32)), axis=1)
    key_norms = jnp.take(query_norms, pattern, axis=0)
    inner_dots = jnp.einsum(
        "qdi,qndj->qinj", query_tiles, key_tiles, preferred_element_type=jnp.float32
    )
    distance = query_norms[:, :, None, None] + key_norms[:, None, :, :] - 2.0 * inner_dots
    query_pos = (
        jnp.arange(block_count, dtype=jnp.int32)[:, None] * block_len
        + jnp.arange(block_len, dtype=jnp.int32)[None, :]
    )
    key_pos = (
        pattern[:, :, None] * block_len + jnp.arange(block_len, dtype=jnp.int32)[None, None, :]
    )
    allowed = (key_pos[:, None, :, :] < length) | (
        key_pos[:, None, :, :] == query_pos[:, :, None, None]
    )
    factor = sharp_head / math.sqrt(head_size)
    weights = jnp.where(allowed, jnp.exp(-factor * distance), 0.0)
    totals = jnp.sum(weights, axis=(2, 3))
    softmax = weights / totals[:, :, None, None]
    softmax_low = softmax.astype(jnp.bfloat16)
    mixed_out = jnp.einsum(
        "qinj,qndj->qdi", softmax_low, key_tiles, preferred_element_type=jnp.float32
    )
    attended = jnp.transpose(mixed_out, (1, 0, 2)).reshape(head_size, seq_total)
    return (attended, softmax, softmax_low, distance)


def head_backward(query_head, cotangent, softmax, softmax_low, sharp_head, pattern):
    head_size, seq_total = query_head.shape
    block_count, fanout = pattern.shape
    block_len = seq_total // block_count
    query_tiles = jnp.transpose(query_head.reshape(head_size, block_count, block_len), (1, 0, 2))
    key_tiles = jnp.take(query_tiles, pattern, axis=0)
    co_tiles = jnp.transpose(cotangent.reshape(head_size, block_count, block_len), (1, 0, 2))
    prob_grad = jnp.einsum(
        "qdi,qndj->qinj", co_tiles, key_tiles, preferred_element_type=jnp.float32
    )
    row_inner = jnp.sum(softmax * prob_grad, axis=(2, 3))
    score_grad = softmax * (prob_grad - row_inner[:, :, None, None])
    factor = sharp_head / math.sqrt(head_size)
    coefficient = (-2.0 * factor * score_grad).astype(jnp.bfloat16)
    coef_wide = coefficient.astype(jnp.float32)
    row_total = jnp.sum(coef_wide, axis=(2, 3))
    col_total = jnp.sum(coef_wide, axis=1)
    query_part = query_tiles.astype(jnp.float32) * row_total[:, None, :] - jnp.einsum(
        "qinj,qndj->qdi", coefficient, key_tiles, preferred_element_type=jnp.float32
    )
    key_part = key_tiles.astype(jnp.float32) * col_total[:, :, None, :] - jnp.einsum(
        "qinj,qdi->qndj", coefficient, query_tiles, preferred_element_type=jnp.float32
    )
    key_part = key_part + jnp.einsum(
        "qinj,qdi->qndj", softmax_low, co_tiles, preferred_element_type=jnp.float32
    )
    selector = (
        pattern[:, :, None] == jnp.arange(block_count, dtype=jnp.int32)[None, None, :]
    ).astype(jnp.float32)
    spread = jnp.einsum("qnk,qndj->kdj", selector, key_part, precision=lax.Precision.HIGHEST)
    total_grad = jnp.transpose(query_part + spread, (1, 0, 2)).reshape(head_size, seq_total)
    return (total_grad, score_grad)


def shards(inputs, w_query, sharpness, pattern, lengths, probes, start_vector):
    tokens = inputs[0]
    probe_rows = probes[0]
    length = lengths[0]
    rows_here = tokens.shape[0]
    position = lax.axis_index("seq") * rows_here + jnp.arange(rows_here, dtype=jnp.int32)
    masked = jnp.where((position < length)[:, None], probe_rows, jnp.zeros_like(probe_rows))
    row_share = w_query.shape[0] // lax.axis_size("dp")
    own_rows = lax.dynamic_slice_in_dim(w_query, lax.axis_index("dp") * row_share, row_share, 0)
    row_band = lax.all_gather(own_rows, "seq", axis=1, tiled=True)
    w_full = lax.all_gather(row_band, "dp", axis=0, tiled=True)
    contract = (((0,), (1,)), ((), ()))
    query_cols = lax.dot_general(
        w_full, tokens, contract, preferred_element_type=jnp.float32
    ).astype(jnp.bfloat16)
    first_cols = lax.dot_general(
        w_full, masked, contract, preferred_element_type=jnp.float32
    ).astype(jnp.bfloat16)
    query_heads, first_heads = (
        lax.all_to_all(query_cols, "seq", split_axis=0, concat_axis=1, tiled=True),
        lax.all_to_all(first_cols, "seq", split_axis=0, concat_axis=1, tiled=True),
    )
    local_heads = sharpness.shape[0]
    seq_total = query_heads.shape[1]
    inner_here = local_heads * DH
    query_stack = query_heads.reshape(local_heads, DH, seq_total)
    first_stack = first_heads.reshape(local_heads, DH, seq_total)

    def first_pass(head_items):
        query_head, cot_head, sharp_head = head_items
        attended, softmax, softmax_low, distance = head_forward(
            query_head, sharp_head, pattern, length
        )
        grad_one, score_grad = head_backward(
            query_head, cot_head, softmax, softmax_low, sharp_head, pattern
        )
        sharp_part = jnp.sum(score_grad * distance) * (-1.0 / math.sqrt(DH))
        return (attended.astype(jnp.bfloat16), grad_one, sharp_part, softmax, softmax_low)

    attended, grad_one, sharp_parts, softmax, softmax_low = lax.map(
        first_pass, (query_stack, first_stack, sharpness)
    )
    term_one = jnp.sum(grad_one * first_stack.astype(jnp.float32))
    back_att, back_grad = (
        lax.all_to_all(
            attended.reshape(inner_here, seq_total), "seq", split_axis=1, concat_axis=0, tiled=True
        ),
        lax.all_to_all(
            grad_one.astype(jnp.bfloat16).reshape(inner_here, seq_total),
            "seq",
            split_axis=1,
            concat_axis=0,
            tiled=True,
        ),
    )
    branch = lax.dot_general(back_att, w_full, contract, preferred_element_type=jnp.float32).astype(
        jnp.bfloat16
    )
    probe_vjp = lax.dot_general(
        back_grad, w_full, contract, preferred_element_type=jnp.float32
    ).astype(jnp.bfloat16)
    second_cols = lax.dot_general(
        w_full, probe_vjp, contract, preferred_element_type=jnp.float32
    ).astype(jnp.bfloat16)
    second_heads = lax.all_to_all(second_cols, "seq", split_axis=0, concat_axis=1, tiled=True)
    second_stack = second_heads.reshape(local_heads, DH, seq_total)

    def second_pass(head_items):
        query_head, cot_head, sharp_head, saved_soft, saved_low = head_items
        grad_two, score_grad = head_backward(
            query_head, cot_head, saved_soft, saved_low, sharp_head, pattern
        )
        return grad_two

    grad_two = lax.map(second_pass, (query_stack, second_stack, sharpness, softmax, softmax_low))
    term_two = jnp.sum(grad_two * first_stack.astype(jnp.float32))
    term_vec = jnp.stack([term_one, term_two]) / (length.astype(jnp.float32) * INNER)
    scale_down = 1.0 / (lax.axis_size("dp") * seq_total * DH)
    term_total = lax.psum(term_vec, "seq")
    sharp_total = lax.psum(sharp_parts, "dp")
    logdet_terms = term_total.reshape(1, 2)
    sharp_grad = sharp_total * scale_down
    w_wide = w_query.astype(jnp.float32)
    column = jnp.dot(start_vector, w_wide, precision=lax.Precision.HIGHEST)
    image_part = jnp.dot(w_wide, column, precision=lax.Precision.HIGHEST)
    image_vec, column_sq = lax.psum((image_part, jnp.sum(jnp.square(column))), "seq")
    spec_vector = image_vec / jnp.sqrt(jnp.mean(jnp.square(image_vec)) + 1e-06)
    spec_norm = jnp.sqrt(jnp.sum(jnp.square(image_vec)) / (column_sq + 1e-06)).reshape(1)
    return (branch[None], probe_vjp[None], logdet_terms, sharp_grad, spec_vector, spec_norm)


def solution(mesh):
    placed = (
        P("dp", "seq", None),
        P(None, "seq"),
        P("seq"),
        P(),
        P("dp"),
        P("dp", "seq", None),
        P(),
    )
    return jax.shard_map(
        shards,
        mesh=mesh,
        in_specs=placed,
        out_specs=(P("dp", "seq", None), P("dp", "seq", None), P("dp", None), P("seq"), P(), P()),
        check_vma=False,
    )
```

profile of v0, /device:TPU:0, one launch (start us, length us, event | category | flops | bytes accessed | tf_op | source)
XLA Modules:
  0.0 406.6 jit_solution(14362392530298967292)
XLA Ops:
  9.2 54.5 %all-gather.3.cloned.1.call-done = bf16[512,2048]{1,0:T(8,128)(2,1)} async-done(((bf16[512,256]{1,0:T(8,128)(2,1)}), bf16[512,2048]{1,0:T(8,128)(2,1)}) %all-gather.3.cloned.1.call-update) | async-done | bytes 2097168 | tf_op jit(solution)/shard_map/all_gather | solution.py:89
  64.4 57.3 %all-gather.5.cloned.1.call-done = bf16[2048,2048]{1,0:T(8,128)(2,1)} async-done(((bf16[512,2048]{1,0:T(8,128)(2,1)}), bf16[2048,2048]{1,0:T(8,128)(2,1)}) %all-gather.5.cloned.1.call-update) | async-done | bytes 8388624 | tf_op jit(solution)/shard_map/all_gather | solution.py:90
  121.8 6.7 %convolution_convert_fusion.3 = bf16[2048,128]{1,0:T(8,128)(2,1)} fusion(bf16[2048,2048]{1,0:T(8,128)(2,1)} %all-gather.5.cloned.1.call-done, bf16[1,128,2048]{2,1,0:T(8,128)(2,1)} %param.18, pred[128]{0:T(512)(128)(4,1)S(1)} %add_compare_fusion), kind=kOutput, calls=%fused_computation.112 | convolution fusion | flops 1074266112 | bytes 9437312 | tf_op jit(solution)/shard_map/dot_general | solution.py:95
  128.4 5.5 %all-to-all-start.1 = ((bf16[8,256,128]{2,1,0:T(8,128)(2,1)}), bf16[8,256,128]{2,1,0:T(8,128)(2,1)S(1)}, u32[]{:S(2)}, u32[]{:S(2)}) async-start(bf16[8,256,128]{2,1,0:T(8,128)(2,1)} %bitcast.59), calls=%async_computation.1 | async-start | bytes 1048576 | tf_op jit(solution)/shard_map/all_to_all | solution.py:100
  133.9 6.6 %convolution_convert_fusion.4 = bf16[2048,128]{1,0:T(8,128)(2,1)} fusion(bf16[2048,2048]{1,0:T(8,128)(2,1)} %all-gather.5.cloned.1.call-done, bf16[1,128,2048]{2,1,0:T(8,128)(2,1)S(1)} %copy-done.6), kind=kOutput, calls=%fused_computation.113 | convolution fusion | flops 1074003968 | bytes 9437184 | tf_op jit(solution)/shard_map/dot_general | solution.py:92
  140.5 8.3 %all-to-all-done.1 = bf16[8,256,128]{2,1,0:T(8,128)(2,1)S(1)} async-done(((bf16[8,256,128]{2,1,0:T(8,128)(2,1)}), bf16[8,256,128]{2,1,0:T(8,128)(2,1)S(1)}, u32[]{:S(2)}, u32[]{:S(2)}) %all-to-all-start.1) | async-done | bytes 524320 | tf_op jit(solution)/shard_map/all_to_all | solution.py:100
  148.8 3.6 all-to-all-start
  153.9 13.3 %all-to-all-done = bf16[8,256,128]{2,1,0:T(8,128)(2,1)S(1)} async-done(((bf16[8,256,128]{2,1,0:T(8,128)(2,1)}), bf16[8,256,128]{2,1,0:T(8,128)(2,1)S(1)}, u32[]{:S(2)}, u32[]{:S(2)}) %all-to-all-start) | async-done | bytes 524320 | tf_op jit(solution)/shard_map/all_to_all | solution.py:99
  169.6 93.9 %while.32 = (s32[]{:T(128)}, bf16[4,64,1024]{2,1,0:T(8,128)(2,1)}, f32[4,64,1024]{2,1,0:T(8,128)}, f32[4]{0:T(128)S(1)}, f32[4,8,128,2,128]{2,4,3,1,0:T(8,128)},...) while((s32[]{:T(128)}, bf16[4,64,1024]{2,1,0:T(8,128)(2,1)}, ...), condition=%wide.region_7.9_spmd, body=%wide.region_0.8_spmd.sunk | while | flops 229250400 | bytes 22127492 | solution.py:119
  175.3 2.6 fusion.116
  179.5 2.1 convolution_bitcast_fusion.13
  181.6 2.5 multiply_reduce_fusion.8
  198.8 2.6 fusion.116
  203.0 2.1 convolution_bitcast_fusion.13
  205.1 2.5 multiply_reduce_fusion.8
  222.3 2.6 fusion.116
  226.4 2.1 convolution_bitcast_fusion.13
  228.5 2.5 multiply_reduce_fusion.8
  245.7 2.6 fusion.116
  249.9 2.1 convolution_bitcast_fusion.13
  252.0 2.5 multiply_reduce_fusion.8
  265.8 3.6 all-to-all-start.3
  271.0 13.2 %all-to-all-done.3 = bf16[256,8,128]{2,0,1:T(8,128)(2,1)S(1)} async-done(((bf16[256,8,128]{2,0,1:T(8,128)(2,1)}), bf16[256,8,128]{2,0,1:T(8,128)(2,1)S(1)}, u32[]{:S(2)}, u32[]{:S(2)}) %all-to-all-start.3) | async-done | bytes 524320 | tf_op jit(solution)/shard_map/all_to_all | solution.py:127
  284.1 3.7 all-to-all-start.2
  287.8 6.3 %convolution_convert_fusion.1 = bf16[128,2048]{1,0:T(8,128)(2,1)S(1)} fusion(bf16[2048,128]{1,0:T(8,128)(2,1)S(1)} %bitcast.324, bf16[2048,2048]{1,0:T(8,128)(2,1)} %all-gather.5.cloned.1.call-done), kind=kOutput, calls=%fused_computation.110 | convolution fusion | flops 1074003968 | bytes 9437184 | tf_op jit(solution)/shard_map/dot_general | solution.py:138
  294.9 6.6 %convolution_convert_fusion = bf16[2048,128]{1,0:T(8,128)(2,1)} fusion(bf16[2048,2048]{1,0:T(8,128)(2,1)} %all-gather.5.cloned.1.call-done, bf16[128,2048]{1,0:T(8,128)(2,1)S(1)} %convolution_convert_fusion.1), kind=kOutput, calls=%fused_computation.109 | convolution fusion | flops 1074003968 | bytes 9437184 | tf_op jit(solution)/shard_map/dot_general | solution.py:141
  302.4 5.0 %all-to-all-start.4 = ((bf16[8,256,128]{2,1,0:T(8,128)(2,1)}), bf16[8,256,128]{2,1,0:T(8,128)(2,1)S(1)}, u32[]{:S(2)}, u32[]{:S(2)}) async-start(bf16[8,256,128]{2,1,0:T(8,128)(2,1)} %bitcast.68), calls=%async_computation.4 | async-start | bytes 1048576 | tf_op jit(solution)/shard_map/all_to_all | solution.py:144
  309.7 5.9 %psum.29 = f32[4]{0:T(128)S(1)} all-reduce(f32[4]{0:T(128)S(1)} %get-tuple-element.254), channel_id=1, replica_groups=mesh['dp'=4,'seq'=8] {'dp'}, use_global_device_ids=true, to_apply=%region_16.18 | all-reduce | flops 4 | bytes 32 | tf_op jit(solution)/shard_map/psum | solution.py:159
  316.1 7.1 %fusion.59 = bf16[1,128,2048]{2,1,0:T(8,128)(2,1)} fusion(bf16[2048,128]{1,0:T(8,128)(2,1)S(1)} %bitcast.323, bf16[2048,2048]{1,0:T(8,128)(2,1)} %all-gather.5.cloned.1.call-done), kind=kOutput, calls=%fused_computation.114 | convolution fusion | flops 1074003968 | bytes 9437184 | tf_op jit(solution)/shard_map/dot_general | solution.py:135
  325.7 43.0 %while.33 = (s32[]{:T(128)}, f32[4,64,1024]{2,1,0:T(8,128)}, bf16[4,64,1024]{2,1,0:T(8,128)(2,1)}, f32[4]{0:T(128)}, f32[4,8,128,2,128]{2,4,3,1,0:T(8,128)}, /*i...) while((s32[]{:T(128)}, f32[4,64,1024]{2,1,0:T(8,128)}, ...), condition=%wide.region_13.15_spmd, body=%wide.region_9.14_spmd.sunk | while | flops 150336784 | bytes 13932365 | solution.py:154
  368.7 2.3 fusion.60
  372.4 23.0 %all-reduce = (f32[1,2]{1,0:T(1,128)}, f32[2048]{0:T(1024)S(1)}, f32[]{:T(128)}) all-reduce(f32[1,2]{1,0:T(1,128)S(1)} %fusion.67, f32[2048]{0:T(1024)} %bitcast.334, f32[]{:T(128)} %multiply_reduce_fusion.4), channel_id=1, replica_groups=mesh['dp'=4,'seq'=8] {'seq'}, use_global_device_ids=true, to_apply=%region_15.17 | all-reduce | flops 2051 | bytes 16408 | tf_op jit(solution)/shard_map/psum | solution.py:158
  (279 shorter events, 116.1 us)
Async XLA Ops:
  7.2 1.2 copy-start
  7.2 56.5 %all-gather.3.cloned.1.call-start = ((), (), s32[]{:S(2)}) async-start(), calls=%async_computation.5 | async-start | bytes 2359296 | tf_op jit(solution)/shard_map/all_gather | solution.py:89
  9.1 112.6 %all-gather.5.cloned.1.call-start = ((), (), s32[]{:S(2)}) async-start(), calls=%async_computation.6 | async-start | bytes 10485760 | tf_op jit(solution)/shard_map/all_gather | solution.py:90
  64.4 69.5 %copy-start.6 = (bf16[1,128,2048]{2,1,0:T(8,128)(2,1)S(1)}, bf16[1,128,2048]{2,1,0:T(8,128)(2,1)}, u32[]{:S(2)}) copy-start(bf16[1,128,2048]{2,1,0:T(8,128)(2,1)} %param.13) | copy-start | bytes 1572868
  128.4 20.4 %all-to-all-start.1 = ((bf16[8,256,128]{2,1,0:T(8,128)(2,1)}), bf16[8,256,128]{2,1,0:T(8,128)(2,1)S(1)}, u32[]{:S(2)}, u32[]{:S(2)}) async-start(bf16[8,256,128]{2,1,0:T(8,128)(2,1)} %bitcast.59), calls=%async_computation.1 | async-start | bytes 1048576 | tf_op jit(solution)/shard_map/all_to_all | solution.py:100
  140.5 29.1 %copy-start.4 = (s32[8,2]{0,1:T(2,128)S(1)}, s32[8,2]{0,1:T(2,128)}, u32[]{:S(2)}) copy-start(s32[8,2]{0,1:T(2,128)} %param.16) | copy-start | bytes 196
  148.8 18.3 %all-to-all-start = ((bf16[8,256,128]{2,1,0:T(8,128)(2,1)}), bf16[8,256,128]{2,1,0:T(8,128)(2,1)S(1)}, u32[]{:S(2)}, u32[]{:S(2)}) async-start(bf16[8,256,128]{2,1,0:T(8,128)(2,1)} %bitcast.55), calls=%async_computation | async-start | bytes 1048576 | tf_op jit(solution)/shard_map/all_to_all | solution.py:99
  263.5 6.0 %copy-start.5 = (f32[2048]{0:T(1024)S(1)}, f32[2048]{0:T(1024)}, u32[]{:S(2)}) copy-start(f32[2048]{0:T(1024)} %param.19) | copy-start | bytes 24580
  263.5 6.5 %copy-start.3 = (bf16[4,64,1024]{2,1,0:T(8,128)(2,1)S(1)}, bf16[4,64,1024]{2,1,0:T(8,128)(2,1)}, u32[]{:S(2)}) copy-start(bf16[4,64,1024]{2,1,0:T(8,128)(2,1)} %get-tuple-element.249) | copy-start | bytes 1572868
  265.8 18.3 %all-to-all-start.3 = ((bf16[256,8,128]{2,0,1:T(8,128)(2,1)}), bf16[256,8,128]{2,0,1:T(8,128)(2,1)S(1)}, u32[]{:S(2)}, u32[]{:S(2)}) async-start(bf16[256,8,128]{2,0,1:T(8,128)(2,1)} %copy.129), calls=%async_computation.3 | async-start | bytes 1048576 | tf_op jit(solution)/shard_map/all_to_all | solution.py:127
  284.1 18.3 %all-to-all-start.2 = ((bf16[256,8,128]{2,0,1:T(8,128)(2,1)}), bf16[256,8,128]{2,0,1:T(8,128)(2,1)S(1)}, u32[]{:S(2)}, u32[]{:S(2)}) async-start(bf16[256,8,128]{2,0,1:T(8,128)(2,1)} %copy.128), calls=%async_computation.2 | async-start | bytes 1048576 | tf_op jit(solution)/shard_map/all_to_all | solution.py:124
  294.1 0.8 copy-start.2
  302.4 20.8 %all-to-all-start.4 = ((bf16[8,256,128]{2,1,0:T(8,128)(2,1)}), bf16[8,256,128]{2,1,0:T(8,128)(2,1)S(1)}, u32[]{:S(2)}, u32[]{:S(2)}) async-start(bf16[8,256,128]{2,1,0:T(8,128)(2,1)} %bitcast.68), calls=%async_computation.4 | async-start | bytes 1048576 | tf_op jit(solution)/shard_map/all_to_all | solution.py:144
  325.7 43.0 %copy-start.1 = (f32[4,64,1024]{2,1,0:T(8,128)S(1)}, f32[4,64,1024]{2,1,0:T(8,128)}, u32[]{:S(2)}) copy-start(f32[4,64,1024]{2,1,0:T(8,128)} %get-tuple-element.250) | copy-start | bytes 3145732
Sparse Core Ops, SparseCore 0:
  10.6 53.0 all-gather.2
  65.3 56.4 all-gather.4
where the time goes:
time: 408 us; the launch traced here: 407 us
  waiting for transfers between devices  148 us (36%)
  matrix products  91.8 us (22%)
  local copies, waits for them, and re-layouts  50.4 us (12%)
  other arithmetic  37.3 us (9%)
  blocking collectives  29 us (7%)
  starting transfers between devices  21.6 us (5%)
  between operations  18 us (4%)
  loops' own time  11.1 us (3%)
    all_gather x1, waiting for transfers between devices, shards(): w_full = lax.all_gather(row_band, 'dp', axis=0, tiled=True)  57.3 us
    all_gather x1, waiting for transfers between devices, shards(): row_band = lax.all_gather(own_rows, 'seq', axis=1, tiled=True)  54.5 us
    psum x1, blocking collectives, shards(): term_total = lax.psum(term_vec, 'seq')  23 us
    dot_general x8, matrix products, head_backward(): jnp.einsum('qdi,qndj->qinj', co_tiles, key_tiles, preferred_element_type=...  17.4 us
    reduce_sum x8, other arithmetic, head_backward(): row_total = jnp.sum(coef_wide, axis=(2, 3))  14.1 us
    dot_general x8, matrix products, head_backward(): jnp.einsum('qinj,qdi->qndj', softmax_low, co_tiles, preferred_element_typ...  13.8 us
    all_to_all x1, waiting for transfers between devices, shards(): lax.all_to_all(query_cols, 'seq', split_axis=0, concat_axis=1, tiled=True)  13.3 us
    all_to_all x1, waiting for transfers between devices, shards(): lax.all_to_all(grad_one.astype(jnp.bfloat16).reshape(inner_here, seq_tota...  13.2 us
  transfers between devices with their start and end apart: 7, of which 6 were waited for; matrix products, arithmetic and copies ran while one was open for 8% of the time, Pallas kernels for 0%

commit v1 on v0

v1 whole, which is shorter than its diff:
```python
import functools
import math

import jax
import jax.numpy as jnp
from jax import lax
from jax.experimental import pallas as pl
from jax.experimental.pallas import tpu as pltpu
from jax.sharding import PartitionSpec as P

DH = 64
F32 = jnp.float32
BF16 = jnp.bfloat16


def dot(a, b, ca, cb):
    return lax.dot_general(a, b, (((ca,), (cb,)), ((), ())), preferred_element_type=F32)


def attention_kernel(heads, q_ref, c_ref, sharp_ref, pat_ref, len_ref, back_ref, stat_ref,
                     grad, cols):
    blocks, width, span = q_ref.shape
    length = len_ref[0]

    def prepare(i, carry):
        grad[i] = jnp.zeros((width, span), F32)
        q = q_ref[i].astype(F32)
        c = c_ref[i].astype(F32)
        rows = [jnp.sum((q * q)[h * DH:(h + 1) * DH], axis=0, keepdims=True) for h in range(heads)]
        rows += [jnp.sum((q * c)[h * DH:(h + 1) * DH], axis=0, keepdims=True) for h in range(heads)]
        if 2 * heads < 8:
            rows.append(jnp.zeros((8 - 2 * heads, span), F32))
        cols[i] = jnp.transpose(jnp.concatenate(rows, axis=0))
        return carry

    lax.fori_loop(0, blocks, prepare, 0)
    stat_ref[...] = jnp.zeros_like(stat_ref)
    key_at = lax.broadcasted_iota(jnp.int32, (span, span), 0)
    query_at = lax.broadcasted_iota(jnp.int32, (span, span), 1)
    tail = (lax.broadcasted_iota(jnp.int32, (16, 2 * span), 1) < span).astype(F32).astype(BF16)

    def block(i, carry):
        other = pat_ref[i, 1]
        allowed = jnp.concatenate(
            [(i * span + key_at < length) | (key_at == query_at), other * span + key_at < length],
            axis=0)
        for h in range(heads):
            hs = slice(h * DH, (h + 1) * DH)
            q = q_ref[i, hs, :]
            c = c_ref[i, hs, :]
            keys = jnp.concatenate([q, q_ref[other, hs, :]], axis=1)
            key_cots = jnp.concatenate([c, c_ref[other, hs, :]], axis=1)
            qc = jnp.concatenate([q, c], axis=1)
            both = dot(keys, qc, 0, 0)
            inner = both[:, :span]
            prob_grad = both[:, span:]
            cross = dot(key_cots, q, 0, 0)
            qf = q.astype(F32)
            cf = c.astype(F32)
            norm_row = jnp.sum(qf * qf, axis=0, keepdims=True)
            pair_row = jnp.sum(qf * cf, axis=0, keepdims=True)
            norm_col = jnp.concatenate([cols[i, :, h:h + 1], cols[other, :, h:h + 1]], axis=0)
            pair_col = jnp.concatenate(
                [cols[i, :, heads + h:heads + h + 1], cols[other, :, heads + h:heads + h + 1]], axis=0)
            factor = sharp_ref[h] * (1.0 / math.sqrt(DH))
            distance = norm_row + norm_col - 2.0 * inner
            weights = jnp.where(allowed, jnp.exp(-factor * distance), 0.0)
            total = jnp.sum(weights, axis=0, keepdims=True)
            soft = weights * (1.0 / total)
            low = soft.astype(BF16)
            row_inner = jnp.sum(soft * prob_grad, axis=0, keepdims=True)
            score = soft * (prob_grad - row_inner)
            stat_ref[h:h + 1, :] += jnp.sum(score * distance, axis=0, keepdims=True)
            coef = (-2.0 * factor * score).astype(BF16)
            row_total = jnp.sum(coef.astype(F32), axis=0, keepdims=True)
            gap = pair_row + pair_col - cross - prob_grad
            gap_mean = jnp.sum(soft * gap, axis=0, keepdims=True)
            adj = (-2.0 * factor * (soft * (gap - gap_mean))).astype(BF16)
            mixed = jnp.concatenate([coef, low], axis=1)
            left = dot(keys, mixed, 1, 0)
            back_ref[0, i, hs, :] = left[:, span:].astype(BF16)
            adjoint = dot(jnp.concatenate([keys, key_cots], axis=1),
                          jnp.concatenate([adj, low], axis=0), 1, 0)
            back_ref[2, i, hs, :] = adjoint.astype(BF16)
            lhs = jnp.concatenate([jnp.concatenate([-q, c], axis=1), tail], axis=0)
            right = dot(lhs, mixed, 1, 1)
            key_part = keys.astype(F32) * right[DH:DH + 1, :] + right[:DH]
            grad[i, hs, :] += qf * row_total - left[:, :span] + key_part[:, :span]
            grad[other, hs, :] += key_part[:, span:]
        return carry

    lax.fori_loop(0, blocks, block, 0)

    def finish(i, term):
        back_ref[1, i] = grad[i].astype(BF16)
        return term + jnp.sum(grad[i] * c_ref[i].astype(F32), axis=0, keepdims=True)

    stat_ref[heads:heads + 1, :] = lax.fori_loop(0, blocks, finish, jnp.zeros((1, span), F32))


def attention(q, c, sharpness, pattern, lengths):
    blocks, width, span = q.shape
    heads = sharpness.shape[0]
    smem = pl.BlockSpec(memory_space=pltpu.SMEM)
    vmem = pl.BlockSpec(memory_space=pltpu.VMEM)
    return pl.pallas_call(
        functools.partial(attention_kernel, heads),
        out_shape=(jax.ShapeDtypeStruct((3, blocks, width, span), BF16),
                   jax.ShapeDtypeStruct((heads + 1, span), F32)),
        in_specs=[vmem, vmem, smem, smem, smem],
        out_specs=(vmem, vmem),
        scratch_shapes=[pltpu.VMEM((blocks, width, span), F32),
                        pltpu.VMEM((blocks, span, max(8, 2 * heads)), F32)],
        compiler_params=pltpu.CompilerParams(vmem_limit_bytes=40 * 1024 * 1024),
        name="attention",
    )(q, c, sharpness, pattern, lengths)


def shards(inputs, w_query, sharpness, pattern, lengths, probes, start_vector):
    tokens = inputs[0]
    probe_rows = probes[0]
    length = lengths[0]
    rows_here = tokens.shape[0]
    groups = lax.axis_size("seq")
    position = lax.axis_index("seq") * rows_here + jnp.arange(rows_here, dtype=jnp.int32)
    masked = jnp.where((position < length)[:, None], probe_rows, jnp.zeros_like(probe_rows))
    row_share = w_query.shape[0] // lax.axis_size("dp")
    inner_here = w_query.shape[1]
    inner = inner_here * groups
    own_rows = lax.dynamic_slice_in_dim(w_query, lax.axis_index("dp") * row_share, row_share, 0)
    row_band = lax.all_gather(own_rows, "seq", axis=1, tiled=True)
    w_full = lax.all_gather(row_band, "dp", axis=0, tiled=True)
    w_wide = w_query.astype(F32)
    column = jnp.dot(start_vector, w_wide, precision=lax.Precision.HIGHEST)
    image_part = jnp.dot(w_wide, column, precision=lax.Precision.HIGHEST)
    both = jnp.concatenate([tokens, masked], axis=0)
    contract = (((0,), (1,)), ((), ()))
    cols = lax.dot_general(w_full, both, contract, preferred_element_type=F32).astype(BF16)
    sent = cols.reshape(groups, inner_here, 2 * rows_here)
    got = lax.all_to_all(sent, "seq", split_axis=0, concat_axis=0, tiled=True)
    q = got[:, :, :rows_here]
    c = got[:, :, rows_here:]
    back, stats = attention(q, c, sharpness, pattern, lengths)
    home = lax.all_to_all(back, "seq", split_axis=1, concat_axis=1, tiled=True)
    home = home.reshape(3, inner, rows_here)
    branch = lax.dot_general(home[0], w_full, contract, preferred_element_type=F32).astype(BF16)
    probe_vjp = lax.dot_general(home[1], w_full, contract, preferred_element_type=F32).astype(BF16)
    second = lax.dot_general(w_full, probe_vjp, contract, preferred_element_type=F32).astype(BF16)
    heads = sharpness.shape[0]
    term_two = jnp.sum(second.astype(F32) * home[2].astype(F32))
    term_one = jnp.sum(stats[heads])
    seq_total = groups * rows_here
    term_vec = jnp.stack([term_one, term_two]) / (length.astype(F32) * inner)
    scale_down = 1.0 / (lax.axis_size("dp") * seq_total * DH)
    sharp_parts = jnp.sum(stats[:heads], axis=1) * (-1.0 / math.sqrt(DH))
    sharp_grad = lax.psum(sharp_parts, "dp") * scale_down
    term_total, image_vec, column_sq = lax.psum(
        (term_vec, image_part, jnp.sum(jnp.square(column))), "seq")
    spec_vector = image_vec / jnp.sqrt(jnp.mean(jnp.square(image_vec)) + 1e-06)
    spec_norm = jnp.sqrt(jnp.sum(jnp.square(image_vec)) / (column_sq + 1e-06)).reshape(1)
    return (branch[None], probe_vjp[None], term_total.reshape(1, 2), sharp_grad, spec_vector, spec_norm)


def solution(mesh):
    placed = (
        P("dp", "seq", None),
        P(None, "seq"),
        P("seq"),
        P(),
        P("dp"),
        P("dp", "seq", None),
        P(),
    )
    return jax.shard_map(
        shards,
        mesh=mesh,
        in_specs=placed,
        out_specs=(P("dp", "seq", None), P("dp", "seq", None), P("dp", None), P("seq"), P(), P()),
        check_vma=False,
    )
```

time: 408 us -> 271 us (0.66)
  matrix products: 91.8 us -> 28.6 us
  local copies, waits for them, and re-layouts: 50.4 us -> 3.79 us
  other arithmetic: 37.3 us -> 5.57 us
  waiting for transfers between devices: 148 us -> 165 us
  Pallas kernels: 0 us -> 14 us
  starting transfers between devices: 21.6 us -> 9.35 us
  loops' own time: 11.1 us -> 0 us
    dot_general x53 -> x4, matrix products: 89.8 us -> 27.1 us  [the longest x1 7.12 us: shards(): lax.dot_general(home[0], w_full, contract, preferred_element_type=F32)]
    all_to_all x5 -> x2, waiting for transfers between devices: 35.7 us -> 54 us  [the longest x1 27.9 us: shards(): home = lax.all_to_all(back, 'seq', split_axis=1, concat_axis=1, tiled=True)]
    reduce_sum x13 -> x2, other arithmetic: 16.5 us -> 0.72 us  [the longest x1 0.6 us: shards(): term_one = jnp.sum(stats[heads])]
    pallas_call x0 -> x1, Pallas kernels: none -> 14 us  [attention(): pl.pallas_call(functools.partial(attention_kernel, heads), out_shape=(jax...]
    all_to_all x5 -> x2, starting transfers between devices: 21.5 us -> 9.27 us  [the longest x1 5.64 us: shards(): got = lax.all_to_all(sent, 'seq', split_axis=0, concat_axis=0, tiled=True)]
    dynamic_update_slice x8 -> x0, other arithmetic: 11.7 us -> none  [shards(): lax.map(first_pass, (query_stack, first_stack, sharpness))]
    another operation x2 -> x0, loops' own time: 11.1 us -> none  [the longest x1 8.06 us: shards(): lax.map(first_pass, (query_stack, first_stack, sharpness))]
    dynamic_slice x8 -> x0, local copies, waits for them, and re-layouts: 9.95 us -> none  [shards(): lax.map(first_pass, (query_stack, first_stack, sharpness))]
  transfers between devices with their start and end apart: 7 -> 4, of which waited for: 6 -> 4; matrix products, arithmetic and copies ran while one was open for 8% -> 2% of each run, Pallas kernels for 0% -> 0%
where the time goes in v1:
time: 271 us
  waiting for transfers between devices  165 us (61%)
  matrix products  28.6 us (11%)
  blocking collectives  26.6 us (10%)
  between operations  18 us (7%)
  Pallas kernels  14 us (5%)
  starting transfers between devices  9.35 us (3%)
  other arithmetic  5.57 us (2%)
  local copies, waits for them, and re-layouts  3.79 us (1%)
    all_gather x1, waiting for transfers between devices, shards(): w_full = lax.all_gather(row_band, 'dp', axis=0, tiled=True)  56.2 us
    all_gather x1, waiting for transfers between devices, shards(): row_band = lax.all_gather(own_rows, 'seq', axis=1, tiled=True)  54.5 us
    all_to_all x1, waiting for transfers between devices, shards(): home = lax.all_to_all(back, 'seq', split_axis=1, concat_axis=1, tiled=True)  27.9 us
    all_to_all x1, waiting for transfers between devices, shards(): got = lax.all_to_all(sent, 'seq', split_axis=0, concat_axis=0, tiled=True)  26.1 us
    psum x1, blocking collectives, shards(): lax.psum((term_vec, image_part, jnp.sum(jnp.square(column))), 'seq')  20.6 us
    pallas_call x1, Pallas kernels, attention(): pl.pallas_call(functools.partial(attention_kernel, heads), out_shape=(jax...  14 us
    dot_general x1, matrix products, shards(): lax.dot_general(home[0], w_full, contract, preferred_element_type=F32)  7.12 us
    dot_general x1, matrix products, shards(): lax.dot_general(w_full, both, contract, preferred_element_type=F32)  7.08 us
  transfers between devices with their start and end apart: 4, of which 4 were waited for; matrix products, arithmetic and copies ran while one was open for 2% of the time, Pallas kernels for 0%

profile of v1, /device:TPU:0, one launch (start us, length us, event | category | flops | bytes accessed | tf_op | source)
XLA Modules:
  0.0 270.6 jit_solution(11867094837395640650)
XLA Ops:
  7.2 0.0 all-gather.3.cloned.1.call-start
  7.2 1.2 copy-done
  8.4 0.7 constant_dynamic-slice_fusion
  9.1 0.0 all-gather.3.cloned.1.call-update
  9.1 0.0 all-gather.5.cloned.1.call-start
  9.2 54.5 %all-gather.3.cloned.1.call-done = bf16[512,2048]{1,0:T(8,128)(2,1)} async-done(((bf16[512,256]{1,0:T(8,128)(2,1)}), bf16[512,2048]{1,0:T(8,128)(2,1)}) %all-gather.3.cloned.1.call-update) | async-done | bytes 2097168 | tf_op jit(solution)/shard_map/all_gather | solution.py:131
  64.4 1.1 bitcast_select_fusion
  65.6 56.2 %all-gather.5.cloned.1.call-done = bf16[2048,2048]{1,0:T(8,128)(2,1)} async-done(((bf16[512,2048]{1,0:T(8,128)(2,1)}), bf16[2048,2048]{1,0:T(8,128)(2,1)}) %all-gather.5.cloned.1.call-update) | async-done | bytes 8388624 | tf_op jit(solution)/shard_map/all_gather | solution.py:132
  121.8 7.1 %convolution_convert_fusion = bf16[2048,256]{1,0:T(8,128)(2,1)} fusion(bf16[2048,2048]{1,0:T(8,128)(2,1)} %all-gather.5.cloned.1.call-done, bf16[128,2048]{1,0:T(8,128)(2,1)S(1)} %bitcast_select_fusion, bf16[128,2048]{1,0:T(8,128)(2,1)} %bitcast.42), kind=kOutput, calls=%fused_computation | convolution fusion | flops 2150105088 | bytes 10485760 | tf_op jit(solution)/shard_map/dot_general | solution.py:138
  128.8 5.6 %all-to-all-start = ((bf16[8,256,256]{2,1,0:T(8,128)(2,1)}), bf16[8,256,256]{2,1,0:T(8,128)(2,1)S(1)}, u32[]{:S(2)}, u32[]{:S(2)}) async-start(bf16[8,256,256]{2,1,0:T(8,128)(2,1)} %bitcast.3), calls=%async_computation | async-start | bytes 2097152 | tf_op jit(solution)/shard_map/all_to_all | solution.py:140
  134.5 0.1 copy.14.pat_ref
  134.6 26.1 %all-to-all-done = bf16[8,256,256]{2,1,0:T(8,128)(2,1)S(1)} async-done(((bf16[8,256,256]{2,1,0:T(8,128)(2,1)}), bf16[8,256,256]{2,1,0:T(8,128)(2,1)S(1)}, u32[]{:S(2)}, u32[]{:S(2)}) %all-to-all-start) | async-done | bytes 1048608 | tf_op jit(solution)/shard_map/all_to_all | solution.py:140
  160.7 0.3 fusion.12
  160.9 14.0 %attention.1 = (bf16[3,8,256,128]{3,2,1,0:T(8,128)(2,1)S(1)}, f32[5,128]{1,0:T(8,128)S(1)}) custom-call(bf16[8,256,128]{2,1,0:T(8,128)(2,1)S(1)} %get-tuple-element.17.q_ref, bf16[8,256,128]{2,1,0:T(8,128)(2,1)S(1)} %get-tuple-element.16.c_ref, f32[4]{0:T(128)S(1)} %copy-done.1, s32[8,2]{1,0:T(8,128)S(1)} %copy.14.pat_ref, s32[1]{0:T(128)} %copy.16.len_ref), custom_call_target="tpu_custom_call" | custom-call | tf_op jit(solution)/shard_map/attention/pallas_call | solution.py:106
  175.0 1.4 copy.15
  176.4 3.6 %all-to-all-start.1 = ((bf16[3,8,256,128]{3,2,0,1:T(8,128)(2,1)}), bf16[3,8,256,128]{3,2,0,1:T(8,128)(2,1)S(1)}, u32[]{:S(2)}, u32[]{:S(2)}) async-start(bf16[3,8,256,128]{3,2,0,1:T(8,128)(2,1)} %copy.15), calls=%async_computation.1 | async-start | bytes 3145728 | tf_op jit(solution)/shard_map/all_to_all | solution.py:144
  180.0 0.5 fusion.13
  180.5 0.6 multiply_reduce_fusion.1
  181.1 0.9 fusion.7
  182.0 0.1 slice_reduce_fusion
  182.2 6.0 %psum.29 = f32[4]{0:T(128)S(1)} all-reduce(f32[4]{0:T(128)S(1)} %broadcast_multiply_fusion.1), channel_id=1, replica_groups=mesh['dp'=4,'seq'=8] {'dp'}, use_global_device_ids=true, to_apply=%region_4.5 | all-reduce | flops 4 | bytes 32 | tf_op jit(solution)/shard_map/psum | solution.py:156
  188.1 0.6 slice_reduce_fusion.1
  188.7 0.5 broadcast_multiply_fusion
  189.3 27.9 %all-to-all-done.1 = bf16[3,8,256,128]{3,2,0,1:T(8,128)(2,1)S(1)} async-done(((bf16[3,8,256,128]{3,2,0,1:T(8,128)(2,1)}), bf16[3,8,256,128]{3,2,0,1:T(8,128)(2,1)S(1)}, u32[]{:S(2)}, u32[]{:S(2)}) %all-to-all-start.1) | async-done | bytes 1572896 | tf_op jit(solution)/shard_map/all_to_all | solution.py:144
  217.2 0.1 fusion.11
  217.3 6.3 %convolution_convert_fusion.2 = bf16[128,2048]{1,0:T(8,128)(2,1)S(1)} fusion(bf16[2048,128]{1,0:T(8,128)(2,1)S(1)} %bitcast.36, bf16[2048,2048]{1,0:T(8,128)(2,1)} %all-gather.5.cloned.1.call-done), kind=kOutput, calls=%fused_computation.4 | convolution fusion | flops 1074003968 | bytes 9437184 | tf_op jit(solution)/shard_map/dot_general | solution.py:147
  223.7 6.6 %fusion.6 = f32[]{:T(128)} fusion(bf16[2048,128]{1,0:T(8,128)(2,1)S(1)} %bitcast.38, bf16[2048,2048]{1,0:T(8,128)(2,1)} %all-gather.5.cloned.1.call-done, bf16[128,2048]{1,0:T(8,128)(2,1)S(1)} %convolution_convert_fusion.2), kind=kOutput, calls=%fused_computation.10 | convolution fusion | flops 1075052544 | bytes 9437188 | tf_op jit(solution)/shard_map/dot_general | solution.py:148
  230.3 1.4 fusion.9
  231.7 20.6 %all-reduce = (f32[1,2]{1,0:T(1,128)}, f32[2048]{0:T(1024)S(1)}, f32[]{:T(128)}) all-reduce(f32[1,2]{1,0:T(1,128)S(1)} %fusion.9, f32[2048]{0:T(1024)S(1)} %bitcast.39, f32[]{:T(128)} %multiply_reduce_fusion.1), channel_id=1, replica_groups=mesh['dp'=4,'seq'=8] {'seq'}, use_global_device_ids=true, to_apply=%region_2.3 | all-reduce | flops 2051 | bytes 16408 | tf_op jit(solution)/shard_map/psum | solution.py:157
  252.2 0.6 multiply_reduce_fusion
  254.9 0.6 broadcast_divide_fusion
  255.5 7.1 %fusion.2 = bf16[1,128,2048]{2,1,0:T(8,128)(2,1)} fusion(bf16[2048,128]{1,0:T(8,128)(2,1)S(1)} %bitcast.35, bf16[2048,2048]{1,0:T(8,128)(2,1)} %all-gather.5.cloned.1.call-done), kind=kOutput, calls=%fused_computation.6 | convolution fusion | flops 1074003968 | bytes 9437184 | tf_op jit(solution)/shard_map/dot_general | solution.py:146
  (12 shorter events, 0.1 us)
Async XLA Ops:
  7.2 1.2 copy-start
  7.2 56.5 %all-gather.3.cloned.1.call-start = ((), (), s32[]{:S(2)}) async-start(), calls=%async_computation.2 | async-start | bytes 2359296 | tf_op jit(solution)/shard_map/all_gather | solution.py:131
  9.1 112.6 %all-gather.5.cloned.1.call-start = ((), (), s32[]{:S(2)}) async-start(), calls=%async_computation.3 | async-start | bytes 10485760 | tf_op jit(solution)/shard_map/all_gather | solution.py:132
  121.8 12.7 %copy-start.4 = (s32[8,2]{0,1:T(2,128)S(1)}, s32[8,2]{0,1:T(2,128)}, u32[]{:S(2)}) copy-start(s32[8,2]{0,1:T(2,128)} %param.10) | copy-start | bytes 196
  121.8 39.2 %copy-start.1 = (f32[4]{0:T(128)S(1)}, f32[4]{0:T(128)}, u32[]{:S(2)}) copy-start(f32[4]{0:T(128)} %sharp_ref.1) | copy-start | bytes 52
  128.8 51.2 %copy-start.3 = (f32[2048]{0:T(1024)S(1)}, f32[2048]{0:T(1024)}, u32[]{:S(2)}) copy-start(f32[2048]{0:T(1024)} %param.13) | copy-start | bytes 24580
  128.8 31.8 %all-to-all-start = ((bf16[8,256,256]{2,1,0:T(8,128)(2,1)}), bf16[8,256,256]{2,1,0:T(8,128)(2,1)S(1)}, u32[]{:S(2)}, u32[]{:S(2)}) async-start(bf16[8,256,256]{2,1,0:T(8,128)(2,1)} %bitcast.3), calls=%async_computation | async-start | bytes 2097152 | tf_op jit(solution)/shard_map/all_to_all | solution.py:140
  176.4 40.8 %all-to-all-start.1 = ((bf16[3,8,256,128]{3,2,0,1:T(8,128)(2,1)}), bf16[3,8,256,128]{3,2,0,1:T(8,128)(2,1)S(1)}, u32[]{:S(2)}, u32[]{:S(2)}) async-start(bf16[3,8,256,128]{3,2,0,1:T(8,128)(2,1)} %copy.15), calls=%async_computation.1 | async-start | bytes 3145728 | tf_op jit(solution)/shard_map/all_to_all | solution.py:144
  223.7 38.9 %copy-start.2 = (bf16[128,2048]{1,0:T(8,128)(2,1)}, bf16[128,2048]{1,0:T(8,128)(2,1)S(1)}, u32[]{:S(2)}) copy-start(bf16[128,2048]{1,0:T(8,128)(2,1)S(1)} %convolution_convert_fusion.2) | copy-start | bytes 1572868
Sparse Core Ops, SparseCore 0:
  10.6 53.0 all-gather.2
  65.3 56.4 all-gather.4

commit v2 on v1

--- a/solution.py
+++ b/solution.py
@@ -116,36 +116,207 @@
     )(q, c, sharpness, pattern, lengths)
 
 
+def gather_kernel(ndp, groups, x_ref, p_ref, w_ref, len_ref, start_ref, w_out, got, image_ref,
+                  norm_ref, both, outbox, acc, recv, send, a2a_recv, a2a_send):
+    span, depth = x_ref.shape
+    width = w_ref.shape[1]
+    lines, rows = groups // 2, depth // ndp
+    ys = ndp // 2
+    me, d = lax.axis_index("seq"), lax.axis_index("dp")
+    z, x = me // 2, me % 2
+    y, core = d // 2, d % 2
+
+    def seq_id(s):
+        return {"seq": s, "dp": d}
+
+    def dp_id(t):
+        return {"seq": me, "dp": t}
+
+    barrier = pltpu.get_barrier_semaphore()
+    for k in range(1, groups):
+        pl.semaphore_signal(barrier, inc=1, device_id=seq_id((me + k) % groups),
+                            device_id_type=pl.DeviceIdType.MESH)
+    pl.semaphore_signal(barrier, inc=1, device_id=dp_id(d + 1 - 2 * core),
+                        device_id_type=pl.DeviceIdType.MESH)
+    for k in range(1, ys):
+        pl.semaphore_signal(barrier, inc=1, device_id=dp_id(((y + k) % ys) * 2 + core),
+                            device_id_type=pl.DeviceIdType.MESH)
+    pl.semaphore_wait(barrier, groups + ys - 1)
+
+    def piece(s, owner, kind, target, own=False):
+        at = pl.ds(pl.multiple_of(owner * rows, rows), rows)
+        src = w_ref.at[at] if own else w_out.at[s, at]
+        return pltpu.make_async_remote_copy(
+            src_ref=src, dst_ref=w_out.at[s, at], send_sem=send.at[kind, s],
+            recv_sem=recv.at[owner, s], device_id=target, device_id_type=pl.DeviceIdType.MESH)
+
+    def landed(s, owner):
+        at = pl.ds(pl.multiple_of(owner * rows, rows), rows)
+        pltpu.make_async_copy(w_out.at[s, at], w_out.at[s, at], recv.at[owner, s]).wait()
+
+    up, down, across = seq_id((me + 2) % groups), seq_id((me + groups - 2) % groups), seq_id(me + 1 - 2 * x)
+    mate = dp_id(d + 1 - 2 * core)
+
+    def order(t):
+        p, side = t // 2, t % 2
+        m = jnp.minimum(z, lines - 1 - z)
+        near = jnp.where(p % 2 == 1, z + (p + 1) // 2, z - p // 2)
+        far = jnp.where(2 * z < lines, p, lines - 1 - p)
+        zs = jnp.where(p <= 2 * m, near, far)
+        xs = (x + side) % 2
+        return zs * 2 + xs, zs, xs
+
+    pl.when(z + 1 < lines)(lambda: piece(me, d, 0, up, True).start())
+    pl.when(z > 0)(lambda: piece(me, d, 1, down, True).start())
+    piece(me, d, 2, across, True).start()
+    w_out[me] = w_ref[...]
+    both[:span] = x_ref[...]
+    valid = me * span + lax.broadcasted_iota(jnp.int32, (span, 1), 0) < len_ref[0]
+    both[span:] = jnp.where(valid, p_ref[...].astype(F32), 0.0).astype(BF16)
+    acc[...] = jnp.zeros_like(acc)
+    norm_ref[...] = jnp.zeros_like(norm_ref)
+
+    def stage_a(t):
+        s, zs, xs = order(t)
+        landed(s, d)
+
+        @pl.when(xs == x)
+        def _():
+            pl.when((zs < z) & (z + 1 < lines))(lambda: piece(s, d, 0, up).start())
+            pl.when((zs > z) & (z > 0))(lambda: piece(s, d, 1, down).start())
+            piece(s, d, 2, across).start()
+
+        for k in range(1, ys):
+            piece(s, d, 3 + k, dp_id(((y + k) % ys) * 2 + core)).start()
+        piece(s, d, 3, mate).start()
+
+    def stage_b(t):
+        s, zs, xs = order(t)
+        for k in range(1, ys):
+            owner = ((y + k) % ys) * 2 + core
+            landed(s, owner)
+            piece(s, owner, 2 + ys + k, mate).start()
+
+    def out_copy(s):
+        return pltpu.make_async_remote_copy(
+            src_ref=outbox.at[s], dst_ref=got.at[me], send_sem=a2a_send.at[s],
+            recv_sem=a2a_recv.at[me], device_id=seq_id(s), device_id_type=pl.DeviceIdType.MESH)
+
+    def stage_c(t):
+        s, zs, xs = order(t)
+
+        @pl.when(t > 0)
+        def _():
+            for k in range(ys):
+                landed(s, ((y + k) % ys) * 2 + 1 - core)
+
+        w = w_out[s]
+        res = jnp.transpose(dot(both[...], w, 1, 0)).astype(BF16)
+
+        @pl.when(t > 0)
+        def _():
+            outbox[s] = res
+            out_copy(s).start()
+
+        @pl.when(t == 0)
+        def _():
+            got[me] = res
+
+        step = 256
+        def col_body(r, total):
+            at = pl.ds(pl.multiple_of(r * step, step), step)
+            part = w_out[s, at, :].astype(F32) * start_ref[at, :]
+            return total + jnp.sum(part, axis=0, keepdims=True)
+
+        column = lax.fori_loop(0, depth // step, col_body, jnp.zeros((1, width), F32))
+        norm_ref[...] += column * column
+
+        def image_body(r, carry):
+            at = pl.ds(pl.multiple_of(r * step, step), step)
+            acc[at, :] += w_out[s, at, :].astype(F32) * column
+            return carry
+
+        lax.fori_loop(0, depth // step, image_body, 0)
+
+    lag_b, lag_c = 2, 3
+
+    def tick(t, carry):
+        pl.when((t > 0) & (t < groups))(lambda: stage_a(t))
+        pl.when((t - lag_b > 0) & (t - lag_b < groups))(lambda: stage_b(t - lag_b))
+        pl.when(t - lag_c >= 0)(lambda: stage_c(t - lag_c))
+        return carry
+
+    lax.fori_loop(0, groups + lag_c, tick, 0)
+    image_ref[...] = jnp.sum(acc[...], axis=1, keepdims=True)
+
+    def drain(t, carry):
+        s, zs, xs = order(t)
+        pl.when((xs == x) & (zs <= z) & (z + 1 < lines))(lambda: piece(s, d, 0, up).wait_send())
+        pl.when((xs == x) & (zs >= z) & (z > 0))(lambda: piece(s, d, 1, down).wait_send())
+        pl.when(xs == x)(lambda: piece(s, d, 2, across).wait_send())
+
+        @pl.when(t > 0)
+        def _():
+            for k in range(1, ys):
+                piece(s, d, 3 + k, mate).wait_send()
+                piece(s, d, 2 + ys + k, mate).wait_send()
+            piece(s, d, 3, mate).wait_send()
+            out_copy(s).wait_send()
+            pltpu.make_async_copy(got.at[s], got.at[s], a2a_recv.at[s]).wait()
+
+        return carry
+
+    lax.fori_loop(0, groups, drain, 0)
+
+
+def gather_project(ndp, groups, tokens, probe_rows, w_query, lengths, start_vector):
+    span, depth = tokens.shape
+    width = w_query.shape[1]
+    smem = pl.BlockSpec(memory_space=pltpu.SMEM)
+    vmem = pl.BlockSpec(memory_space=pltpu.VMEM)
+    return pl.pallas_call(
+        functools.partial(gather_kernel, ndp, groups),
+        out_shape=(jax.ShapeDtypeStruct((groups, depth, width), BF16),
+                   jax.ShapeDtypeStruct((groups, width, 2 * span), BF16),
+                   jax.ShapeDtypeStruct((depth, 1), F32),
+                   jax.ShapeDtypeStruct((1, width), F32)),
+        in_specs=[vmem, vmem, vmem, smem, vmem],
+        out_specs=(vmem, vmem, vmem, vmem),
+        scratch_shapes=[pltpu.VMEM((2 * span, depth), BF16),
+                        pltpu.VMEM((groups, width, 2 * span), BF16),
+                        pltpu.VMEM((depth, width), F32),
+                        pltpu.SemaphoreType.DMA((ndp, groups)),
+                        pltpu.SemaphoreType.DMA((2 + ndp, groups)),
+                        pltpu.SemaphoreType.DMA((groups,)),
+                        pltpu.SemaphoreType.DMA((groups,))],
+        compiler_params=pltpu.CompilerParams(collective_id=0, has_side_effects=True,
+                                             vmem_limit_bytes=56 * 1024 * 1024),
+        name="gather_project",
+    )(tokens, probe_rows, w_query, lengths, start_vector.reshape(depth, 1))
+
+
 def shards(inputs, w_query, sharpness, pattern, lengths, probes, start_vector):
     tokens = inputs[0]
     probe_rows = probes[0]
     length = lengths[0]
     rows_here = tokens.shape[0]
     groups = lax.axis_size("seq")
-    position = lax.axis_index("seq") * rows_here + jnp.arange(rows_here, dtype=jnp.int32)
-    masked = jnp.where((position < length)[:, None], probe_rows, jnp.zeros_like(probe_rows))
-    row_share = w_query.shape[0] // lax.axis_size("dp")
     inner_here = w_query.shape[1]
     inner = inner_here * groups
-    own_rows = lax.dynamic_slice_in_dim(w_query, lax.axis_index("dp") * row_share, row_share, 0)
-    row_band = lax.all_gather(own_rows, "seq", axis=1, tiled=True)
-    w_full = lax.all_gather(row_band, "dp", axis=0, tiled=True)
-    w_wide = w_query.astype(F32)
-    column = jnp.dot(start_vector, w_wide, precision=lax.Precision.HIGHEST)
-    image_part = jnp.dot(w_wide, column, precision=lax.Precision.HIGHEST)
-    both = jnp.concatenate([tokens, masked], axis=0)
-    contract = (((0,), (1,)), ((), ()))
-    cols = lax.dot_general(w_full, both, contract, preferred_element_type=F32).astype(BF16)
-    sent = cols.reshape(groups, inner_here, 2 * rows_here)
-    got = lax.all_to_all(sent, "seq", split_axis=0, concat_axis=0, tiled=True)
+    w_all, got, image, norms = gather_project(
+        lax.axis_size("dp"), groups, tokens, probe_rows, w_query, lengths, start_vector)
     q = got[:, :, :rows_here]
     c = got[:, :, rows_here:]
     back, stats = attention(q, c, sharpness, pattern, lengths)
     home = lax.all_to_all(back, "seq", split_axis=1, concat_axis=1, tiled=True)
-    home = home.reshape(3, inner, rows_here)
-    branch = lax.dot_general(home[0], w_full, contract, preferred_element_type=F32).astype(BF16)
-    probe_vjp = lax.dot_general(home[1], w_full, contract, preferred_element_type=F32).astype(BF16)
-    second = lax.dot_general(w_full, probe_vjp, contract, preferred_element_type=F32).astype(BF16)
+    def spread(block):
+        return lax.dot_general(block, w_all, (((0, 1), (0, 2)), ((), ())),
+                               preferred_element_type=F32).astype(BF16)
+
+    branch = spread(home[0])
+    probe_vjp = spread(home[1])
+    second = lax.dot_general(w_all, probe_vjp, (((1,), (1,)), ((), ())),
+                             preferred_element_type=F32).astype(BF16)
     heads = sharpness.shape[0]
     term_two = jnp.sum(second.astype(F32) * home[2].astype(F32))
     term_one = jnp.sum(stats[heads])
@@ -154,8 +325,9 @@
     scale_down = 1.0 / (lax.axis_size("dp") * seq_total * DH)
     sharp_parts = jnp.sum(stats[:heads], axis=1) * (-1.0 / math.sqrt(DH))
     sharp_grad = lax.psum(sharp_parts, "dp") * scale_down
-    term_total, image_vec, column_sq = lax.psum(
-        (term_vec, image_part, jnp.sum(jnp.square(column))), "seq")
+    term_total = lax.psum(term_vec, "seq")
+    image_vec = image.reshape(-1)
+    column_sq = jnp.sum(norms)
     spec_vector = image_vec / jnp.sqrt(jnp.mean(jnp.square(image_vec)) + 1e-06)
     spec_norm = jnp.sqrt(jnp.sum(jnp.square(image_vec)) / (column_sq + 1e-06)).reshape(1)
     return (branch[None], probe_vjp[None], term_total.reshape(1, 2), sharp_grad, spec_vector, spec_norm)

time: 271 us -> 179 us (0.66)
  waiting for transfers between devices: 165 us -> 25 us
  Pallas kernels: 14 us -> 88.5 us
  between operations: 18 us -> 4.54 us
  matrix products: 28.6 us -> 20 us
  starting transfers between devices: 9.35 us -> 3.58 us
    all_gather x2 -> x0, waiting for transfers between devices: 111 us -> none  [the longest x1 56.2 us: shards(): w_full = lax.all_gather(row_band, 'dp', axis=0, tiled=True)]
    pallas_call x0 -> x1, Pallas kernels: none -> 74.5 us  [gather_project(): pl.pallas_call(functools.partial(gather_kernel, ndp, groups), out_shape=(...]
    all_to_all x1 -> x0, waiting for transfers between devices: 26.1 us -> none  [shards(): got = lax.all_to_all(sent, 'seq', split_axis=0, concat_axis=0, tiled=True)]
    dot_general x6 -> x3, matrix products: 28.6 us -> 20 us  [the longest x2 13.4 us: spread(): lax.dot_general(block, w_all, (((0, 1), (0, 2)), ((), ())), preferred_ele...]
    all_to_all x1 -> x0, starting transfers between devices: 5.64 us -> none  [shards(): got = lax.all_to_all(sent, 'seq', split_axis=0, concat_axis=0, tiled=True)]
    all_to_all x1, waiting for transfers between devices: 27.9 us -> 25 us  [shards(): home = lax.all_to_all(back, 'seq', split_axis=1, concat_axis=1, tiled=True)]
  transfers between devices with their start and end apart: 4 -> 1, of which waited for: 4 -> 1; matrix products, arithmetic and copies ran while one was open for 2% -> 2% of each run, Pallas kernels for 0% -> 0%
where the time goes in v2:
time: 179 us
  Pallas kernels  88.5 us (49%)
  blocking collectives  25.9 us (14%)
  waiting for transfers between devices  25 us (14%)
  matrix products  20 us (11%)
  local copies, waits for them, and re-layouts  6.17 us (3%)
  other arithmetic  5.02 us (3%)
  between operations  4.54 us (3%)
  starting transfers between devices  3.58 us (2%)
    pallas_call x1, Pallas kernels, gather_project(): pl.pallas_call(functools.partial(gather_kernel, ndp, groups), out_shape=(...  74.5 us
    all_to_all x1, waiting for transfers between devices, shards(): home = lax.all_to_all(back, 'seq', split_axis=1, concat_axis=1, tiled=True)  25 us
    psum x1, blocking collectives, shards(): term_total = lax.psum(term_vec, 'seq')  20 us
    pallas_call x1, Pallas kernels, attention(): pl.pallas_call(functools.partial(attention_kernel, heads), out_shape=(jax...  14 us
    dot_general x2, matrix products, spread(): lax.dot_general(block, w_all, (((0, 1), (0, 2)), ((), ())), preferred_ele...  13.4 us
    dot_general x1, matrix products, shards(): lax.dot_general(w_all, probe_vjp, (((1,), (1,)), ((), ())), preferred_ele...  6.58 us
    psum x1, blocking collectives, shards(): sharp_grad = lax.psum(sharp_parts, 'dp') * scale_down  5.96 us
    all_to_all x1, starting transfers between devices, shards(): home = lax.all_to_all(back, 'seq', split_axis=1, concat_axis=1, tiled=True)  3.58 us
  transfers between devices with their start and end apart: 1, of which 1 were waited for; matrix products, arithmetic and copies ran while one was open for 2% of the time, Pallas kernels for 0%

profile of v2, /device:TPU:0, one launch (start us, length us, event | category | flops | bytes accessed | tf_op | source)
XLA Modules:
  0.0 178.8 jit_solution(7607853642551326336)
XLA Ops:
  1.3 0.8 copy.23.pat_ref
  2.0 2.0 %copy.22.start_ref = f32[2048,1]{1,0:T(8,128)} copy(f32[2048,1]{0,1:T(1,128)} %bitcast.46) | data formatting | bytes 16384 | tf_op jit(solution)/shard_map/reshape | solution.py:295
  4.1 74.5 %gather_project.1 = (bf16[8,2048,256]{2,1,0:T(8,128)(2,1)}, bf16[8,256,256]{2,1,0:T(8,128)(2,1)}, f32[2048,1]{1,0:T(8,128)}, f32[1,256]{1,0:T(1,128)}) custom-call(bf16[128,2048]{1,0:T(8,128)(2,1)} %bitcast.44, bf16[128,2048]{1,0:T(8,128)(2,1)} %bitcast.45, bf16[2048,256]{1,0:T(8,128)(2,1)} %w_ref.1, s32[1]{0:T(128)S(6)} %copy.33.len_ref, ...), custom_call_target="tpu_custom_call" | custom-call | tf_op jit(solution)/shard_map/gather_project/pallas_call | solution.py:277
  78.6 0.0 copy-start.1
  78.6 0.0 copy-start.3
  78.6 1.4 fusion.8
  80.0 0.0 copy-start
  80.0 0.6 copy-done
  80.7 14.0 %attention.1 = (bf16[3,8,256,128]{3,2,1,0:T(8,128)(2,1)S(1)}, f32[5,128]{1,0:T(8,128)S(1)}) custom-call(bf16[8,256,128]{2,1,0:T(8,128)(2,1)S(1)} %get-tuple-element.19.q_ref, bf16[8,256,128]{2,1,0:T(8,128)(2,1)S(1)} %get-tuple-element.18.c_ref, f32[4]{0:T(128)S(1)} %copy-done, s32[8,2]{1,0:T(8,128)S(1)} %copy.23.pat_ref, s32[1]{0:T(128)S(6)} %copy.33.len_ref), custom_call_target="tpu_custom_call" | custom-call | tf_op jit(solution)/shard_map/attention/pallas_call | solution.py:106
  94.7 1.3 copy.24
  96.0 3.6 %all-to-all-start = ((bf16[3,8,256,128]{3,2,0,1:T(8,128)(2,1)}), bf16[3,8,256,128]{3,2,0,1:T(8,128)(2,1)S(1)}, u32[]{:S(2)}, u32[]{:S(2)}) async-start(bf16[3,8,256,128]{3,2,0,1:T(8,128)(2,1)} %copy.24), calls=%async_computation | async-start | bytes 3145728 | tf_op jit(solution)/shard_map/all_to_all | solution.py:311
  99.6 0.1 slice_reduce_fusion
  99.7 6.0 %psum.15 = f32[4]{0:T(128)S(1)} all-reduce(f32[4]{0:T(128)S(1)} %broadcast_multiply_fusion.1), channel_id=1, replica_groups=mesh['dp'=4,'seq'=8] {'dp'}, use_global_device_ids=true, to_apply=%region_4.0 | all-reduce | flops 4 | bytes 32 | tf_op jit(solution)/shard_map/psum | solution.py:327
  105.7 0.0 copy-done.1
  105.7 0.9 multiply_reduce_fusion
  107.3 0.0 copy-done.3
  107.3 0.6 reduce_sum.53
  109.2 0.6 slice_reduce_fusion.1
  109.8 0.5 broadcast_multiply_fusion
  110.3 0.9 divide_reduce_fusion
  111.2 25.0 %all-to-all-done = bf16[3,8,256,128]{3,2,0,1:T(8,128)(2,1)S(1)} async-done(((bf16[3,8,256,128]{3,2,0,1:T(8,128)(2,1)}), bf16[3,8,256,128]{3,2,0,1:T(8,128)(2,1)S(1)}, u32[]{:S(2)}, u32[]{:S(2)}) %all-to-all-start) | async-done | bytes 1572896 | tf_op jit(solution)/shard_map/all_to_all | solution.py:311
  136.3 6.3 %fusion.1 = bf16[128,2048]{1,0:T(8,128)(2,1)S(1)} fusion(bf16[8,2048,256]{2,1,0:T(8,128)(2,1)} %get-tuple-element.14, bf16[3,8,256,128]{3,2,0,1:T(8,128)(2,1)S(1)} %all-to-all-done), kind=kOutput, calls=%fused_computation.3 | convolution fusion | flops 1074003968 | bytes 9437184 | tf_op jit(solution)/shard_map/dot_general | solution.py:313
  142.6 0.0 copy-start.2
  142.6 6.6 %fusion.5 = f32[]{:T(128)} fusion(bf16[8,2048,256]{2,1,0:T(8,128)(2,1)} %get-tuple-element.14, bf16[3,8,256,128]{3,2,0,1:T(8,128)(2,1)S(1)} %all-to-all-done, bf16[128,2048]{1,0:T(8,128)(2,1)S(1)} %fusion.1), kind=kOutput, calls=%fused_computation.10 | convolution fusion | flops 1075052544 | bytes 9437188 | tf_op jit(solution)/shard_map/dot_general | solution.py:318
  149.2 1.4 fusion.7
  150.6 20.0 %psum.14 = f32[1,2]{1,0:T(1,128)} all-reduce(f32[1,2]{1,0:T(1,128)S(1)} %fusion.7), channel_id=1, replica_groups=mesh['dp'=4,'seq'=8] {'seq'}, use_global_device_ids=true, to_apply=%region_2.0 | all-reduce | flops 2 | bytes 16 | tf_op jit(solution)/shard_map/psum | solution.py:328
  170.6 7.1 %fusion.2 = bf16[1,128,2048]{2,1,0:T(8,128)(2,1)} fusion(bf16[8,2048,256]{2,1,0:T(8,128)(2,1)} %get-tuple-element.14, bf16[3,8,256,128]{3,2,0,1:T(8,128)(2,1)S(1)} %all-to-all-done), kind=kOutput, calls=%fused_computation.4 | convolution fusion | flops 1074003968 | bytes 9437184 | tf_op jit(solution)/shard_map/dot_general | solution.py:313
  177.7 0.0 copy-done.2
  (1 shorter events, 0.0 us)
Async XLA Ops:
  78.6 27.1 %copy-start.1 = (f32[2048,1]{1,0:T(8,128)S(1)}, f32[2048,1]{1,0:T(8,128)}, u32[]{:S(2)}) copy-start(f32[2048,1]{1,0:T(8,128)} %get-tuple-element.16) | copy-start | bytes 24580
  78.6 28.6 %copy-start.3 = (f32[1,256]{1,0:T(1,128)S(1)}, f32[1,256]{1,0:T(1,128)}, u32[]{:S(2)}) copy-start(f32[1,256]{1,0:T(1,128)} %get-tuple-element.17) | copy-start | bytes 3076
  80.0 0.7 copy-start
  96.0 40.3 %all-to-all-start = ((bf16[3,8,256,128]{3,2,0,1:T(8,128)(2,1)}), bf16[3,8,256,128]{3,2,0,1:T(8,128)(2,1)S(1)}, u32[]{:S(2)}, u32[]{:S(2)}) async-start(bf16[3,8,256,128]{3,2,0,1:T(8,128)(2,1)} %copy.24), calls=%async_computation | async-start | bytes 3145728 | tf_op jit(solution)/shard_map/all_to_all | solution.py:311
  142.6 35.1 %copy-start.2 = (bf16[128,2048]{1,0:T(8,128)(2,1)}, bf16[128,2048]{1,0:T(8,128)(2,1)S(1)}, u32[]{:S(2)}) copy-start(bf16[128,2048]{1,0:T(8,128)(2,1)S(1)} %fusion.1) | copy-start | bytes 1572868

commit v3 on v2

--- a/solution.py
+++ b/solution.py
@@ -17,15 +17,50 @@
     return lax.dot_general(a, b, (((ca,), (cb,)), ((), ())), preferred_element_type=F32)
 
 
-def attention_kernel(heads, q_ref, c_ref, sharp_ref, pat_ref, len_ref, back_ref, stat_ref,
-                     grad, cols):
-    blocks, width, span = q_ref.shape
+def attention_kernel(heads, ndp, qc_ref, w_ref, sharp_ref, pat_ref, len_ref, branch_ref, vjp_ref,
+                     stat_ref, cols, own, other_part, box_a, box_g, home_a, home_g, left_rows,
+                     grad_rows, adjoint_out, w_all, seq_tile, dp_tile, w_sem, a_send, a_recv, g_send,
+                     g_recv, s_send, s_recv, d_send, d_recv):
+    blocks, width, pair = qc_ref.shape
+    span = pair // 2
+    depth = w_all.shape[1]
+    me, d = lax.axis_index("seq"), lax.axis_index("dp")
     length = len_ref[0]
+    mesh_id = pl.DeviceIdType.MESH
+
+    fetch = pltpu.make_async_copy(w_ref, w_all, w_sem)
+    fetch.start()
+    barrier = pltpu.get_barrier_semaphore()
+    for k in range(1, blocks):
+        pl.semaphore_signal(barrier, inc=1, device_id={"seq": (me + k) % blocks, "dp": d},
+                            device_id_type=mesh_id)
+    for k in range(1, ndp):
+        pl.semaphore_signal(barrier, inc=1, device_id={"seq": me, "dp": (d + k) % ndp},
+                            device_id_type=mesh_id)
+
+    def push(src, dst, send, recv, target, t_dp):
+        return pltpu.make_async_remote_copy(
+            src_ref=src, dst_ref=dst, send_sem=send, recv_sem=recv,
+            device_id={"seq": target, "dp": t_dp}, device_id_type=mesh_id)
+
+    def push_a(i):
+        return push(box_a.at[i], home_a.at[me], a_send.at[i], a_recv.at[me], i, d)
+
+    def push_g(i):
+        return push(box_g.at[i], home_g.at[me], g_send.at[i], g_recv.at[me], i, d)
+
+    def push_s(i):
+        return push(seq_tile.at[me], seq_tile.at[me], s_send.at[i], s_recv.at[me], i, d)
+
+    def push_d(j):
+        return push(dp_tile.at[d], dp_tile.at[d], d_send.at[j], d_recv.at[d], me, j)
+
+    def arrived(ref, sem):
+        pltpu.make_async_copy(ref, ref, sem).wait()
 
     def prepare(i, carry):
-        grad[i] = jnp.zeros((width, span), F32)
-        q = q_ref[i].astype(F32)
-        c = c_ref[i].astype(F32)
+        q = qc_ref[i, :, :span].astype(F32)
+        c = qc_ref[i, :, span:].astype(F32)
         rows = [jnp.sum((q * q)[h * DH:(h + 1) * DH], axis=0, keepdims=True) for h in range(heads)]
         rows += [jnp.sum((q * c)[h * DH:(h + 1) * DH], axis=0, keepdims=True) for h in range(heads)]
         if 2 * heads < 8:
@@ -34,23 +69,27 @@
         return carry
 
     lax.fori_loop(0, blocks, prepare, 0)
-    stat_ref[...] = jnp.zeros_like(stat_ref)
+    sharp_at = dp_tile.at[d]
+    sharp_at[...] = jnp.zeros((8, span), F32)
     key_at = lax.broadcasted_iota(jnp.int32, (span, span), 0)
     query_at = lax.broadcasted_iota(jnp.int32, (span, span), 1)
     tail = (lax.broadcasted_iota(jnp.int32, (16, 2 * span), 1) < span).astype(F32).astype(BF16)
-
-    def block(i, carry):
+    pl.semaphore_wait(barrier, blocks + ndp - 2)
+
+    def block(k, carry):
+        i = (me + blocks // 2 + k) % blocks
         other = pat_ref[i, 1]
         allowed = jnp.concatenate(
             [(i * span + key_at < length) | (key_at == query_at), other * span + key_at < length],
             axis=0)
         for h in range(heads):
             hs = slice(h * DH, (h + 1) * DH)
-            q = q_ref[i, hs, :]
-            c = c_ref[i, hs, :]
-            keys = jnp.concatenate([q, q_ref[other, hs, :]], axis=1)
-            key_cots = jnp.concatenate([c, c_ref[other, hs, :]], axis=1)
-            qc = jnp.concatenate([q, c], axis=1)
+            qc = qc_ref[i, hs, :]
+            qc_other = qc_ref[other, hs, :]
+            q = qc[:, :span]
+            c = qc[:, span:]
+            keys = jnp.concatenate([q, qc_other[:, :span]], axis=1)
+            key_cots = jnp.concatenate([c, qc_other[:, span:]], axis=1)
             both = dot(keys, qc, 0, 0)
             inner = both[:, :span]
             prob_grad = both[:, span:]
@@ -70,7 +109,7 @@
             low = soft.astype(BF16)
             row_inner = jnp.sum(soft * prob_grad, axis=0, keepdims=True)
             score = soft * (prob_grad - row_inner)
-            stat_ref[h:h + 1, :] += jnp.sum(score * distance, axis=0, keepdims=True)
+            dp_tile[d, h:h + 1, :] += jnp.sum(score * distance, axis=0, keepdims=True)
             coef = (-2.0 * factor * score).astype(BF16)
             row_total = jnp.sum(coef.astype(F32), axis=0, keepdims=True)
             gap = pair_row + pair_col - cross - prob_grad
@@ -78,42 +117,140 @@
             adj = (-2.0 * factor * (soft * (gap - gap_mean))).astype(BF16)
             mixed = jnp.concatenate([coef, low], axis=1)
             left = dot(keys, mixed, 1, 0)
-            back_ref[0, i, hs, :] = left[:, span:].astype(BF16)
+            box_a[i, 0, hs, :] = left[:, span:].astype(BF16)
             adjoint = dot(jnp.concatenate([keys, key_cots], axis=1),
                           jnp.concatenate([adj, low], axis=0), 1, 0)
-            back_ref[2, i, hs, :] = adjoint.astype(BF16)
+            box_a[i, 1, hs, :] = adjoint.astype(BF16)
             lhs = jnp.concatenate([jnp.concatenate([-q, c], axis=1), tail], axis=0)
             right = dot(lhs, mixed, 1, 1)
             key_part = keys.astype(F32) * right[DH:DH + 1, :] + right[:DH]
-            grad[i, hs, :] += qf * row_total - left[:, :span] + key_part[:, :span]
-            grad[other, hs, :] += key_part[:, span:]
+            own[i, hs, :] = qf * row_total - left[:, :span] + key_part[:, :span]
+            other_part[i, hs, :] = key_part[:, span:]
+        pl.when(i != me)(lambda: push_a(i).start())
         return carry
 
     lax.fori_loop(0, blocks, block, 0)
 
-    def finish(i, term):
-        back_ref[1, i] = grad[i].astype(BF16)
-        return term + jnp.sum(grad[i] * c_ref[i].astype(F32), axis=0, keepdims=True)
-
-    stat_ref[heads:heads + 1, :] = lax.fori_loop(0, blocks, finish, jnp.zeros((1, span), F32))
-
-
-def attention(q, c, sharpness, pattern, lengths):
-    blocks, width, span = q.shape
+    def finish(k, term):
+        m = (me + blocks // 2 + k) % blocks
+
+        def gather(i, total):
+            chosen = jnp.where(pat_ref[i, 1] == m, 1.0, 0.0)
+            return total + other_part[i] * chosen
+
+        if blocks <= 8:
+            g = own[m]
+            for i in range(blocks):
+                g = gather(i, g)
+        else:
+            g = lax.fori_loop(0, blocks, gather, own[m])
+        box_g[m] = g.astype(BF16)
+        pl.when(m != me)(lambda: push_g(m).start())
+        return term + jnp.sum(g * qc_ref[m, :, span:].astype(F32), axis=0, keepdims=True)
+
+    term_one = lax.fori_loop(0, blocks, finish, jnp.zeros((1, span), F32))
+    for k in range(1, ndp):
+        push_d((d + k) % ndp).start()
+    home_a[me] = box_a[me]
+    home_g[me] = box_g[me]
+    fetch.wait()
+
+    def take_a(k, carry):
+        s = (me + k) % blocks
+        pl.when(k > 0)(lambda: arrived(home_a.at[s], a_recv.at[s]))
+        left_rows[s] = jnp.concatenate(
+            [jnp.transpose(home_a[s, 0]), jnp.transpose(home_a[s, 1])], axis=0)
+        return carry
+
+    lax.fori_loop(0, blocks, take_a, 0)
+    step = 256
+
+    def product(rows_ref, r):
+        at = pl.ds(pl.multiple_of(r * step, step), step)
+        total = jnp.zeros((rows_ref.shape[1], step), F32)
+        for s in range(blocks):
+            total = total + dot(rows_ref[s], w_all[s, at, :], 1, 1)
+        return at, total
+
+    def outward(r, carry):
+        at, total = product(left_rows, r)
+        branch_ref[:, at] = total[:span].astype(BF16)
+        adjoint_out[:, at] = total[span:]
+        return carry
+
+    lax.fori_loop(0, depth // step, outward, 0)
+
+    def take_g(k, carry):
+        s = (me + k) % blocks
+        pl.when(k > 0)(lambda: arrived(home_g.at[s], g_recv.at[s]))
+        grad_rows[s] = jnp.transpose(home_g[s])
+        return carry
+
+    lax.fori_loop(0, blocks, take_g, 0)
+
+    def backward(r, term):
+        at, total = product(grad_rows, r)
+        low = total.astype(BF16)
+        vjp_ref[:, at] = low
+        part = low.astype(F32) * adjoint_out[:, at]
+        for n in range(step // span):
+            term = term + jnp.sum(part[:, n * span:(n + 1) * span], axis=0, keepdims=True)
+        return term
+
+    term_two = lax.fori_loop(0, depth // step, backward, jnp.zeros((1, span), F32))
+    seq_tile[me] = jnp.concatenate([term_one, term_two, jnp.zeros((6, span), F32)], axis=0)
+    for k in range(1, blocks):
+        push_s((me + k) % blocks).start()
+    for k in range(1, ndp):
+        j = (d + k) % ndp
+        arrived(dp_tile.at[j], d_recv.at[j])
+        push_d(j).wait_send()
+    for k in range(1, blocks):
+        i = (me + k) % blocks
+        push_a(i).wait_send()
+        push_g(i).wait_send()
+        arrived(seq_tile.at[i], s_recv.at[i])
+        push_s(i).wait_send()
+    stat_ref[:8] = jnp.broadcast_to(
+        jnp.sum(jnp.sum(seq_tile[...], axis=0), axis=1, keepdims=True), (8, span))
+    stat_ref[8:] = jnp.broadcast_to(
+        jnp.sum(jnp.sum(dp_tile[...], axis=0), axis=1, keepdims=True), (8, span))
+
+
+def attention(ndp, qc, w_all, sharpness, pattern, lengths):
+    blocks, width, pair = qc.shape
+    span = pair // 2
+    depth = w_all.shape[1]
     heads = sharpness.shape[0]
     smem = pl.BlockSpec(memory_space=pltpu.SMEM)
     vmem = pl.BlockSpec(memory_space=pltpu.VMEM)
+    sem = pltpu.SemaphoreType.DMA
     return pl.pallas_call(
-        functools.partial(attention_kernel, heads),
-        out_shape=(jax.ShapeDtypeStruct((3, blocks, width, span), BF16),
-                   jax.ShapeDtypeStruct((heads + 1, span), F32)),
-        in_specs=[vmem, vmem, smem, smem, smem],
-        out_specs=(vmem, vmem),
-        scratch_shapes=[pltpu.VMEM((blocks, width, span), F32),
-                        pltpu.VMEM((blocks, span, max(8, 2 * heads)), F32)],
-        compiler_params=pltpu.CompilerParams(vmem_limit_bytes=40 * 1024 * 1024),
+        functools.partial(attention_kernel, heads, ndp),
+        out_shape=(jax.ShapeDtypeStruct((span, depth), BF16),
+                   jax.ShapeDtypeStruct((span, depth), BF16),
+                   jax.ShapeDtypeStruct((16, span), F32)),
+        in_specs=[vmem, pl.BlockSpec(memory_space=pl.ANY), smem, smem, smem],
+        out_specs=(vmem, vmem, vmem),
+        scratch_shapes=[pltpu.VMEM((blocks, span, max(8, 2 * heads)), F32),
+                        pltpu.VMEM((blocks, width, span), F32),
+                        pltpu.VMEM((blocks, width, span), F32),
+                        pltpu.VMEM((blocks, 2, width, span), BF16),
+                        pltpu.VMEM((blocks, width, span), BF16),
+                        pltpu.VMEM((blocks, 2, width, span), BF16),
+                        pltpu.VMEM((blocks, width, span), BF16),
+                        pltpu.VMEM((blocks, 2 * span, width), BF16),
+                        pltpu.VMEM((blocks, span, width), BF16),
+                        pltpu.VMEM((span, depth), F32),
+                        pltpu.VMEM((blocks, depth, width), BF16),
+                        pltpu.VMEM((blocks, 8, span), F32),
+                        pltpu.VMEM((ndp, 8, span), F32),
+                        sem, sem((blocks,)), sem((blocks,)), sem((blocks,)), sem((blocks,)),
+                        sem((blocks,)), sem((blocks,)), sem((ndp,)), sem((ndp,))],
+        compiler_params=pltpu.CompilerParams(collective_id=1, has_side_effects=True,
+                                             vmem_limit_bytes=56 * 1024 * 1024),
         name="attention",
-    )(q, c, sharpness, pattern, lengths)
+    )(qc, w_all, sharpness, pattern, lengths)
 
 
 def gather_kernel(ndp, groups, x_ref, p_ref, w_ref, len_ref, start_ref, w_out, got, image_ref,
@@ -305,27 +442,13 @@
     inner = inner_here * groups
     w_all, got, image, norms = gather_project(
         lax.axis_size("dp"), groups, tokens, probe_rows, w_query, lengths, start_vector)
-    q = got[:, :, :rows_here]
-    c = got[:, :, rows_here:]
-    back, stats = attention(q, c, sharpness, pattern, lengths)
-    home = lax.all_to_all(back, "seq", split_axis=1, concat_axis=1, tiled=True)
-    def spread(block):
-        return lax.dot_general(block, w_all, (((0, 1), (0, 2)), ((), ())),
-                               preferred_element_type=F32).astype(BF16)
-
-    branch = spread(home[0])
-    probe_vjp = spread(home[1])
-    second = lax.dot_general(w_all, probe_vjp, (((1,), (1,)), ((), ())),
-                             preferred_element_type=F32).astype(BF16)
+    branch, probe_vjp, stats = attention(
+        lax.axis_size("dp"), got, w_all, sharpness, pattern, lengths)
     heads = sharpness.shape[0]
-    term_two = jnp.sum(second.astype(F32) * home[2].astype(F32))
-    term_one = jnp.sum(stats[heads])
     seq_total = groups * rows_here
-    term_vec = jnp.stack([term_one, term_two]) / (length.astype(F32) * inner)
+    term_total = stats[:2, 0] / (length.astype(F32) * inner)
     scale_down = 1.0 / (lax.axis_size("dp") * seq_total * DH)
-    sharp_parts = jnp.sum(stats[:heads], axis=1) * (-1.0 / math.sqrt(DH))
-    sharp_grad = lax.psum(sharp_parts, "dp") * scale_down
-    term_total = lax.psum(term_vec, "seq")
+    sharp_grad = stats[8:8 + heads, 0] * (-1.0 / math.sqrt(DH)) * scale_down
     image_vec = image.reshape(-1)
     column_sq = jnp.sum(norms)
     spec_vector = image_vec / jnp.sqrt(jnp.mean(jnp.square(image_vec)) + 1e-06)

time: 179 us -> 141 us (0.79)
  Pallas kernels: 88.5 us -> 123 us
  blocking collectives: 25.9 us -> 0 us
  waiting for transfers between devices: 25 us -> 0 us
  matrix products: 20 us -> 0 us
  starting transfers between devices: 3.58 us -> 0 us
    pallas_call x1, Pallas kernels: 14 us -> 48.9 us  [attention(): pl.pallas_call(functools.partial(attention_kernel, heads, ndp), out_shape...]
    psum x2 -> x0, blocking collectives: 25.9 us -> none  [the longest x1 20 us: shards(): term_total = lax.psum(term_vec, 'seq')]
    all_to_all x1 -> x0, waiting for transfers between devices: 25 us -> none  [shards(): home = lax.all_to_all(back, 'seq', split_axis=1, concat_axis=1, tiled=True)]
    dot_general x3 -> x0, matrix products: 20 us -> none  [the longest x2 13.4 us: spread(): lax.dot_general(block, w_all, (((0, 1), (0, 2)), ((), ())), preferred_ele...]
    unnamed x9 -> x7, local copies, waits for them, and re-layouts: 1.42 us -> 5.2 us
    all_to_all x1 -> x0, starting transfers between devices: 3.58 us -> none  [shards(): home = lax.all_to_all(back, 'seq', split_axis=1, concat_axis=1, tiled=True)]
  transfers between devices with their start and end apart: 1 -> 0, of which waited for: 1 -> 0; matrix products, arithmetic and copies ran while one was open for 2% -> 0% of each run, Pallas kernels for 0% -> 0%
where the time goes in v3:
time: 141 us; the launch traced here: 140 us
  Pallas kernels  123 us (87%)
  local copies, waits for them, and re-layouts  7.25 us (5%)
  other arithmetic  5.02 us (4%)
  between operations  4.49 us (3%)
    pallas_call x1, Pallas kernels, gather_project(): pl.pallas_call(functools.partial(gather_kernel, ndp, groups), out_shape=(...  74.5 us
    pallas_call x1, Pallas kernels, attention(): pl.pallas_call(functools.partial(attention_kernel, heads, ndp), out_shape...  48.9 us
    unnamed x7, local copies, waits for them, and re-layouts  5.2 us

profile of v3, /device:TPU:0, one launch (start us, length us, event | category | flops | bytes accessed | tf_op | source)
XLA Modules:
  0.0 140.2 jit_solution(7639595612709438998)
XLA Ops:
  1.3 2.0 %copy.14.start_ref = f32[2048,1]{1,0:T(8,128)} copy(f32[2048,1]{0,1:T(1,128)} %bitcast.12) | data formatting | bytes 16384 | tf_op jit(solution)/shard_map/reshape | solution.py:432
  3.3 74.5 %gather_project.1 = (bf16[8,2048,256]{2,1,0:T(8,128)(2,1)}, bf16[8,256,256]{2,1,0:T(8,128)(2,1)}, f32[2048,1]{1,0:T(8,128)}, f32[1,256]{1,0:T(1,128)}) custom-call(bf16[128,2048]{1,0:T(8,128)(2,1)} %bitcast.10, bf16[128,2048]{1,0:T(8,128)(2,1)} %bitcast.11, bf16[2048,256]{1,0:T(8,128)(2,1)} %w_ref.1, s32[1]{0:T(128)S(6)} %copy.18.len_ref, ...), custom_call_target="tpu_custom_call" | custom-call | tf_op jit(solution)/shard_map/gather_project/pallas_call | solution.py:414
  77.9 0.0 copy-start
  77.9 0.0 copy-start.1
  77.9 1.4 %copy.15.pat_ref = s32[8,2]{1,0:T(8,128)} copy(s32[8,2]{0,1:T(2,128)} %param.10) | data formatting | bytes 128 | tf_op args[3]
  79.3 48.9 %attention.1 = (bf16[128,2048]{1,0:T(8,128)(2,1)}, bf16[128,2048]{1,0:T(8,128)(2,1)}, f32[16,128]{1,0:T(8,128)}) custom-call(bf16[8,256,256]{2,1,0:T(8,128)(2,1)} %get-tuple-element.13.qc_ref, bf16[8,2048,256]{2,1,0:T(8,128)(2,1)} %get-tuple-element.14.w_ref, f32[4]{0:T(128)} %sharp_ref.1, s32[8,2]{1,0:T(8,128)} %copy.15.pat_ref, s32[1]{0:T(128)S(6)} %copy.18.len_ref), custom_call_target="tpu_custom_call" | custom-call | tf_op jit(solution)/shard_map/attention/pallas_call | solution.py:228
  128.3 1.3 fusion
  129.6 1.3 multiply_reduce_fusion.1
  130.9 0.0 copy-done
  130.9 0.9 multiply_reduce_fusion
  132.4 0.9 divide_reduce_fusion
  133.4 0.0 copy-done.1
  133.4 0.6 reduce_sum.20
  135.3 1.9 %copy.19 = bf16[1,128,2048]{2,1,0:T(8,128)(2,1)} copy(bf16[1,128,2048]{2,1,0:T(8,128)(2,1)} %bitcast.9) | data formatting | bytes 1048576
  137.2 1.9 %copy.20 = bf16[1,128,2048]{2,1,0:T(8,128)(2,1)} copy(bf16[1,128,2048]{2,1,0:T(8,128)(2,1)} %bitcast.8) | data formatting | bytes 1048576
Async XLA Ops:
  77.9 53.0 %copy-start = (f32[2048,1]{1,0:T(8,128)S(1)}, f32[2048,1]{1,0:T(8,128)}, u32[]{:S(2)}) copy-start(f32[2048,1]{1,0:T(8,128)} %get-tuple-element.18) | copy-start | bytes 24580
  77.9 55.5 %copy-start.1 = (f32[1,256]{1,0:T(1,128)S(1)}, f32[1,256]{1,0:T(1,128)}, u32[]{:S(2)}) copy-start(f32[1,256]{1,0:T(1,128)} %get-tuple-element.19) | copy-start | bytes 3076

commit v4 on v3

--- a/solution.py
+++ b/solution.py
@@ -17,8 +17,8 @@
     return lax.dot_general(a, b, (((ca,), (cb,)), ((), ())), preferred_element_type=F32)
 
 
-def attention_kernel(heads, ndp, qc_ref, w_ref, sharp_ref, pat_ref, len_ref, branch_ref, vjp_ref,
-                     stat_ref, cols, own, other_part, box_a, box_g, home_a, home_g, left_rows,
+def attention_kernel(heads, ndp, qc_ref, w_ref, sharp_ref, pat_ref, len_ref, start_ref, branch_ref,
+                     vjp_ref, stat_ref, spec_ref, image, cols, own, other_part, box_a, box_g, home_a, home_g, left_rows,
                      grad_rows, adjoint_out, w_all, seq_tile, dp_tile, w_sem, a_send, a_recv, g_send,
                      g_recv, s_send, s_recv, d_send, d_recv):
     blocks, width, pair = qc_ref.shape
@@ -158,10 +158,24 @@
     def take_a(k, carry):
         s = (me + k) % blocks
         pl.when(k > 0)(lambda: arrived(home_a.at[s], a_recv.at[s]))
-        left_rows[s] = jnp.concatenate(
+        left_rows[s, :2 * span, :] = jnp.concatenate(
             [jnp.transpose(home_a[s, 0]), jnp.transpose(home_a[s, 1])], axis=0)
         return carry
 
+    def split(v):
+        high = v.astype(BF16).astype(F32)
+        mid = (v - high).astype(BF16).astype(F32)
+        rows = [high, mid, v - high - mid, jnp.zeros((13, v.shape[1]), F32)]
+        return jnp.concatenate(rows, axis=0).astype(BF16)
+
+    start_rows = split(start_ref[...])
+
+    def power(s, total):
+        column = jnp.sum(dot(start_rows, w_all[s], 1, 0), axis=0, keepdims=True)
+        left_rows[s, 2 * span:, :] = split(column)
+        return total + column * column
+
+    column_sq = lax.fori_loop(0, blocks, power, jnp.zeros((1, width), F32))
     lax.fori_loop(0, blocks, take_a, 0)
     step = 256
 
@@ -175,7 +189,8 @@
     def outward(r, carry):
         at, total = product(left_rows, r)
         branch_ref[:, at] = total[:span].astype(BF16)
-        adjoint_out[:, at] = total[span:]
+        adjoint_out[:, at] = total[span:2 * span]
+        image[:, at] = jnp.sum(total[2 * span:], axis=0, keepdims=True)
         return carry
 
     lax.fori_loop(0, depth // step, outward, 0)
@@ -197,6 +212,10 @@
             term = term + jnp.sum(part[:, n * span:(n + 1) * span], axis=0, keepdims=True)
         return term
 
+    image_sq = jnp.sum(image[...] * image[...], axis=1, keepdims=True)
+    spec_ref[...] = image[...] / jnp.sqrt(image_sq / depth + 1e-06)
+    norm = jnp.sqrt(image_sq / (jnp.sum(column_sq, axis=1, keepdims=True) + 1e-06))
+    stat_ref[16:] = jnp.broadcast_to(norm, (8, span))
     term_two = lax.fori_loop(0, depth // step, backward, jnp.zeros((1, span), F32))
     seq_tile[me] = jnp.concatenate([term_one, term_two, jnp.zeros((6, span), F32)], axis=0)
     for k in range(1, blocks):
@@ -213,11 +232,11 @@
         push_s(i).wait_send()
     stat_ref[:8] = jnp.broadcast_to(
         jnp.sum(jnp.sum(seq_tile[...], axis=0), axis=1, keepdims=True), (8, span))
-    stat_ref[8:] = jnp.broadcast_to(
+    stat_ref[8:16] = jnp.broadcast_to(
         jnp.sum(jnp.sum(dp_tile[...], axis=0), axis=1, keepdims=True), (8, span))
 
 
-def attention(ndp, qc, w_all, sharpness, pattern, lengths):
+def attention(ndp, qc, w_all, sharpness, pattern, lengths, start_vector):
     blocks, width, pair = qc.shape
     span = pair // 2
     depth = w_all.shape[1]
@@ -229,17 +248,19 @@
         functools.partial(attention_kernel, heads, ndp),
         out_shape=(jax.ShapeDtypeStruct((span, depth), BF16),
                    jax.ShapeDtypeStruct((span, depth), BF16),
-                   jax.ShapeDtypeStruct((16, span), F32)),
-        in_specs=[vmem, pl.BlockSpec(memory_space=pl.ANY), smem, smem, smem],
-        out_specs=(vmem, vmem, vmem),
-        scratch_shapes=[pltpu.VMEM((blocks, span, max(8, 2 * heads)), F32),
+                   jax.ShapeDtypeStruct((24, span), F32),
+                   jax.ShapeDtypeStruct((1, depth), F32)),
+        in_specs=[vmem, pl.BlockSpec(memory_space=pl.ANY), smem, smem, smem, vmem],
+        out_specs=(vmem, vmem, vmem, vmem),
+        scratch_shapes=[pltpu.VMEM((1, depth), F32),
+                        pltpu.VMEM((blocks, span, max(8, 2 * heads)), F32),
                         pltpu.VMEM((blocks, width, span), F32),
                         pltpu.VMEM((blocks, width, span), F32),
                         pltpu.VMEM((blocks, 2, width, span), BF16),
                         pltpu.VMEM((blocks, width, span), BF16),
                         pltpu.VMEM((blocks, 2, width, span), BF16),
                         pltpu.VMEM((blocks, width, span), BF16),
-                        pltpu.VMEM((blocks, 2 * span, width), BF16),
+                        pltpu.VMEM((blocks, 2 * span + 16, width), BF16),
                         pltpu.VMEM((blocks, span, width), BF16),
                         pltpu.VMEM((span, depth), F32),
                         pltpu.VMEM((blocks, depth, width), BF16),
@@ -250,11 +271,22 @@
         compiler_params=pltpu.CompilerParams(collective_id=1, has_side_effects=True,
                                              vmem_limit_bytes=56 * 1024 * 1024),
         name="attention",
-    )(qc, w_all, sharpness, pattern, lengths)
-
-
-def gather_kernel(ndp, groups, x_ref, p_ref, w_ref, len_ref, start_ref, w_out, got, image_ref,
-                  norm_ref, both, outbox, acc, recv, send, a2a_recv, a2a_send):
+    )(qc, w_all, sharpness, pattern, lengths, start_vector.reshape(1, depth))
+
+
+def keep_kernel(a_ref, b_ref, a_out, b_out):
+    a_out[...] = a_ref[...]
+    b_out[...] = b_ref[...]
+
+
+def keep(a, b):
+    vmem = pl.BlockSpec(memory_space=pltpu.VMEM)
+    shape = jax.ShapeDtypeStruct(a.shape, a.dtype)
+    return pl.pallas_call(keep_kernel, out_shape=(shape, shape), in_specs=[vmem, vmem],
+                          out_specs=(vmem, vmem), name="keep")(a, b)
+
+
+def gather_kernel(ndp, groups, x_ref, p_ref, w_ref, len_ref, w_out, got, both, outbox, recv, send, a2a_recv, a2a_send):
     span, depth = x_ref.shape
     width = w_ref.shape[1]
     lines, rows = groups // 2, depth // ndp
@@ -306,12 +338,12 @@
     pl.when(z + 1 < lines)(lambda: piece(me, d, 0, up, True).start())
     pl.when(z > 0)(lambda: piece(me, d, 1, down, True).start())
     piece(me, d, 2, across, True).start()
+    for k in range(1, ys):
+        piece(me, ((y + k) % ys) * 2 + core, 3 + k, across, True).start()
     w_out[me] = w_ref[...]
     both[:span] = x_ref[...]
     valid = me * span + lax.broadcasted_iota(jnp.int32, (span, 1), 0) < len_ref[0]
     both[span:] = jnp.where(valid, p_ref[...].astype(F32), 0.0).astype(BF16)
-    acc[...] = jnp.zeros_like(acc)
-    norm_ref[...] = jnp.zeros_like(norm_ref)
 
     def stage_a(t):
         s, zs, xs = order(t)
@@ -323,8 +355,11 @@
             pl.when((zs > z) & (z > 0))(lambda: piece(s, d, 1, down).start())
             piece(s, d, 2, across).start()
 
-        for k in range(1, ys):
-            piece(s, d, 3 + k, dp_id(((y + k) % ys) * 2 + core)).start()
+        @pl.when(t > 1)
+        def _():
+            for k in range(1, ys):
+                piece(s, d, 3 + k, dp_id(((y + k) % ys) * 2 + core)).start()
+
         piece(s, d, 3, mate).start()
 
     def stage_b(t):
@@ -359,22 +394,6 @@
         def _():
             got[me] = res
 
-        step = 256
-        def col_body(r, total):
-            at = pl.ds(pl.multiple_of(r * step, step), step)
-            part = w_out[s, at, :].astype(F32) * start_ref[at, :]
-            return total + jnp.sum(part, axis=0, keepdims=True)
-
-        column = lax.fori_loop(0, depth // step, col_body, jnp.zeros((1, width), F32))
-        norm_ref[...] += column * column
-
-        def image_body(r, carry):
-            at = pl.ds(pl.multiple_of(r * step, step), step)
-            acc[at, :] += w_out[s, at, :].astype(F32) * column
-            return carry
-
-        lax.fori_loop(0, depth // step, image_body, 0)
-
     lag_b, lag_c = 2, 3
 
     def tick(t, carry):
@@ -384,7 +403,6 @@
         return carry
 
     lax.fori_loop(0, groups + lag_c, tick, 0)
-    image_ref[...] = jnp.sum(acc[...], axis=1, keepdims=True)
 
     def drain(t, carry):
         s, zs, xs = order(t)
@@ -392,10 +410,14 @@
         pl.when((xs == x) & (zs >= z) & (z > 0))(lambda: piece(s, d, 1, down).wait_send())
         pl.when(xs == x)(lambda: piece(s, d, 2, across).wait_send())
 
-        @pl.when(t > 0)
+        @pl.when(t != 1)
         def _():
             for k in range(1, ys):
                 piece(s, d, 3 + k, mate).wait_send()
+
+        @pl.when(t > 0)
+        def _():
+            for k in range(1, ys):
                 piece(s, d, 2 + ys + k, mate).wait_send()
             piece(s, d, 3, mate).wait_send()
             out_copy(s).wait_send()
@@ -406,7 +428,7 @@
     lax.fori_loop(0, groups, drain, 0)
 
 
-def gather_project(ndp, groups, tokens, probe_rows, w_query, lengths, start_vector):
+def gather_project(ndp, groups, tokens, probe_rows, w_query, lengths):
     span, depth = tokens.shape
     width = w_query.shape[1]
     smem = pl.BlockSpec(memory_space=pltpu.SMEM)
@@ -414,14 +436,11 @@
     return pl.pallas_call(
         functools.partial(gather_kernel, ndp, groups),
         out_shape=(jax.ShapeDtypeStruct((groups, depth, width), BF16),
-                   jax.ShapeDtypeStruct((groups, width, 2 * span), BF16),
-                   jax.ShapeDtypeStruct((depth, 1), F32),
-                   jax.ShapeDtypeStruct((1, width), F32)),
-        in_specs=[vmem, vmem, vmem, smem, vmem],
-        out_specs=(vmem, vmem, vmem, vmem),
+                   jax.ShapeDtypeStruct((groups, width, 2 * span), BF16)),
+        in_specs=[vmem, vmem, vmem, smem],
+        out_specs=(vmem, vmem),
         scratch_shapes=[pltpu.VMEM((2 * span, depth), BF16),
                         pltpu.VMEM((groups, width, 2 * span), BF16),
-                        pltpu.VMEM((depth, width), F32),
                         pltpu.SemaphoreType.DMA((ndp, groups)),
                         pltpu.SemaphoreType.DMA((2 + ndp, groups)),
                         pltpu.SemaphoreType.DMA((groups,)),
@@ -429,7 +448,7 @@
         compiler_params=pltpu.CompilerParams(collective_id=0, has_side_effects=True,
                                              vmem_limit_bytes=56 * 1024 * 1024),
         name="gather_project",
-    )(tokens, probe_rows, w_query, lengths, start_vector.reshape(depth, 1))
+    )(tokens, probe_rows, w_query, lengths)
 
 
 def shards(inputs, w_query, sharpness, pattern, lengths, probes, start_vector):
@@ -440,19 +459,18 @@
     groups = lax.axis_size("seq")
     inner_here = w_query.shape[1]
     inner = inner_here * groups
-    w_all, got, image, norms = gather_project(
-        lax.axis_size("dp"), groups, tokens, probe_rows, w_query, lengths, start_vector)
-    branch, probe_vjp, stats = attention(
-        lax.axis_size("dp"), got, w_all, sharpness, pattern, lengths)
+    w_all, got = gather_project(
+        lax.axis_size("dp"), groups, tokens, probe_rows, w_query, lengths)
+    branch, probe_vjp, stats, spec = attention(
+        lax.axis_size("dp"), got, w_all, sharpness, pattern, lengths, start_vector)
+    branch, probe_vjp = keep(branch, probe_vjp)
     heads = sharpness.shape[0]
     seq_total = groups * rows_here
     term_total = stats[:2, 0] / (length.astype(F32) * inner)
     scale_down = 1.0 / (lax.axis_size("dp") * seq_total * DH)
     sharp_grad = stats[8:8 + heads, 0] * (-1.0 / math.sqrt(DH)) * scale_down
-    image_vec = image.reshape(-1)
-    column_sq = jnp.sum(norms)
-    spec_vector = image_vec / jnp.sqrt(jnp.mean(jnp.square(image_vec)) + 1e-06)
-    spec_norm = jnp.sqrt(jnp.sum(jnp.square(image_vec)) / (column_sq + 1e-06)).reshape(1)
+    spec_vector = spec.reshape(-1)
+    spec_norm = stats[16, :1]
     return (branch[None], probe_vjp[None], term_total.reshape(1, 2), sharp_grad, spec_vector, spec_norm)
 
 

time: 141 us -> 134 us (0.950)
  local copies, waits for them, and re-layouts: 7.25 us -> 3.84 us
  between operations: 4.49 us -> 1.3 us
  Pallas kernels: 123 us -> 126 us
  other arithmetic: 5.02 us -> 2.6 us
    unnamed x7 -> x2, local copies, waits for them, and re-layouts: 5.2 us -> 2.64 us
    pallas_call x0 -> x1, Pallas kernels: none -> 2.2 us  [keep(): pl.pallas_call(keep_kernel, out_shape=(shape, shape), in_specs=[vmem, vme...]
    reshape x1 -> x0, local copies, waits for them, and re-layouts: 2.04 us -> none  [gather_project(): start_vector.reshape(depth, 1)]
    reduce_sum x2 -> x0, other arithmetic: 1.47 us -> none  [the longest x1 0.87 us: shards(): spec_vector = image_vec / jnp.sqrt(jnp.mean(jnp.square(image_vec)) + 1e-06)]
where the time goes in v4:
time: 134 us
  Pallas kernels  126 us (94%)
  local copies, waits for them, and re-layouts  3.84 us (3%)
  other arithmetic  2.6 us (2%)
    pallas_call x1, Pallas kernels, gather_project(): pl.pallas_call(functools.partial(gather_kernel, ndp, groups), out_shape=(...  74.5 us
    pallas_call x1, Pallas kernels, attention(): pl.pallas_call(functools.partial(attention_kernel, heads, ndp), out_shape...  49.4 us

profile of v4, /device:TPU:0, one launch (start us, length us, event | category | flops | bytes accessed | tf_op | source)
XLA Modules:
  0.0 133.9 jit_solution(11246198932234758575)
XLA Ops:
  1.3 74.5 %gather_project.1 = (bf16[8,2048,256]{2,1,0:T(8,128)(2,1)}, bf16[8,256,256]{2,1,0:T(8,128)(2,1)}) custom-call(bf16[128,2048]{1,0:T(8,128)(2,1)} %bitcast.9, bf16[128,2048]{1,0:T(8,128)(2,1)} %bitcast.10, bf16[2048,256]{1,0:T(8,128)(2,1)} %w_ref.1, s32[1]{0:T(128)S(6)} %copy.16.len_ref), custom_call_target="tpu_custom_call" | custom-call | tf_op jit(solution)/shard_map/gather_project/pallas_call | solution.py:436
  75.8 1.3 %copy.14.pat_ref = s32[8,2]{1,0:T(8,128)} copy(s32[8,2]{0,1:T(2,128)} %param.10) | data formatting | bytes 128 | tf_op args[3]
  77.1 49.4 %attention.1 = (bf16[128,2048]{1,0:T(8,128)(2,1)}, bf16[128,2048]{1,0:T(8,128)(2,1)}, f32[24,128]{1,0:T(8,128)}, f32[1,2048]{1,0:T(1,128)}) custom-call(bf16[8,256,256]{2,1,0:T(8,128)(2,1)} %get-tuple-element.14.qc_ref, bf16[8,2048,256]{2,1,0:T(8,128)(2,1)} %get-tuple-element.15.w_ref, f32[4]{0:T(128)} %sharp_ref.1, s32[8,2]{1,0:T(8,128)} %copy.14.pat_ref, ...), custom_call_target="tpu_custom_call" | custom-call | tf_op jit(solution)/shard_map/attention/pallas_call | solution.py:247
  126.6 2.2 %keep.1 = (bf16[128,2048]{1,0:T(8,128)(2,1)}, bf16[128,2048]{1,0:T(8,128)(2,1)}) custom-call(bf16[128,2048]{1,0:T(8,128)(2,1)} %get-tuple-element.16.a_ref, bf16[128,2048]{1,0:T(8,128)(2,1)} %get-tuple-element.17.b_ref), custom_call_target="tpu_custom_call" | custom-call | tf_op jit(solution)/shard_map/keep/pallas_call | solution.py:285
  128.8 1.3 fusion
  130.1 1.2 slice.11
  131.3 1.3 multiply_reduce_fusion
  132.6 1.3 copy.17

commit v5 on v4

--- a/solution.py
+++ b/solution.py
@@ -394,7 +394,7 @@
         def _():
             got[me] = res
 
-    lag_b, lag_c = 2, 3
+    lag_b, lag_c = 4, 5
 
     def tick(t, carry):
         pl.when((t > 0) & (t < groups))(lambda: stage_a(t))

time: 134 us -> 137 us (1.022)
  Pallas kernels: 126 us -> 129 us
    pallas_call x1, Pallas kernels: 74.5 us -> 77.3 us  [gather_project(): pl.pallas_call(functools.partial(gather_kernel, ndp, groups), out_shape=(...]
where the time goes in v5:
time: 137 us
  Pallas kernels  129 us (94%)
  local copies, waits for them, and re-layouts  3.84 us (3%)
  other arithmetic  2.6 us (2%)
    pallas_call x1, Pallas kernels, gather_project(): pl.pallas_call(functools.partial(gather_kernel, ndp, groups), out_shape=(...  77.3 us
    pallas_call x1, Pallas kernels, attention(): pl.pallas_call(functools.partial(attention_kernel, heads, ndp), out_shape...  49.6 us

profile of v5, /device:TPU:0, one launch (start us, length us, event | category | flops | bytes accessed | tf_op | source)
XLA Modules:
  0.0 136.9 jit_solution(14962755060026622634)
XLA Ops:
  1.3 77.3 %gather_project.1 = (bf16[8,2048,256]{2,1,0:T(8,128)(2,1)}, bf16[8,256,256]{2,1,0:T(8,128)(2,1)}) custom-call(bf16[128,2048]{1,0:T(8,128)(2,1)} %bitcast.9, bf16[128,2048]{1,0:T(8,128)(2,1)} %bitcast.10, bf16[2048,256]{1,0:T(8,128)(2,1)} %w_ref.1, s32[1]{0:T(128)S(6)} %copy.16.len_ref), custom_call_target="tpu_custom_call" | custom-call | tf_op jit(solution)/shard_map/gather_project/pallas_call | solution.py:436
  78.6 1.3 copy.14.pat_ref
  80.0 49.6 %attention.1 = (bf16[128,2048]{1,0:T(8,128)(2,1)}, bf16[128,2048]{1,0:T(8,128)(2,1)}, f32[24,128]{1,0:T(8,128)}, f32[1,2048]{1,0:T(1,128)}) custom-call(bf16[8,256,256]{2,1,0:T(8,128)(2,1)} %get-tuple-element.14.qc_ref, bf16[8,2048,256]{2,1,0:T(8,128)(2,1)} %get-tuple-element.15.w_ref, f32[4]{0:T(128)} %sharp_ref.1, s32[8,2]{1,0:T(8,128)} %copy.14.pat_ref, ...), custom_call_target="tpu_custom_call" | custom-call | tf_op jit(solution)/shard_map/attention/pallas_call | solution.py:247
  129.6 2.2 %keep.1 = (bf16[128,2048]{1,0:T(8,128)(2,1)}, bf16[128,2048]{1,0:T(8,128)(2,1)}) custom-call(bf16[128,2048]{1,0:T(8,128)(2,1)} %get-tuple-element.16.a_ref, bf16[128,2048]{1,0:T(8,128)(2,1)} %get-tuple-element.17.b_ref), custom_call_target="tpu_custom_call" | custom-call | tf_op jit(solution)/shard_map/keep/pallas_call | solution.py:285
  131.8 1.3 fusion
  133.1 1.2 slice.11
  134.3 1.3 multiply_reduce_fusion
  135.6 1.3 copy.17
